TPU v7x, 32 devices: a whole 2x2x4 slice. The times are simulated.
32 devices in a mesh: groups: 1, ctx: 32 (over z, y, x, core).
Axes of the slice: x: 2, y: 2, z: 4, core: 2. Of those that a mesh axis runs over, the one named last changes fastest.
Arguments:
- prefill_query: bfloat16 [1024, 32, 576], P('groups', 'ctx'), may hold values from -1000 to 1000
- prefill_latent: bfloat16 [1024, 576], P(('groups', 'ctx')), may hold values from -6 to 6
- decode_query: bfloat16 [2, 32, 576], P('groups'), may hold values from -1000 to 1000
- cache: bfloat16 [2, 16384, 576], P('groups', 'ctx'), may hold values from -6 to 6
- lengths: int32 [2], P('groups'), may hold values from 2049 to 16384
- page_table: int32 [64, 2], P('groups'), may hold values from 0 to 31, as said below
Outputs:
- prefill_out: bfloat16 [1024, 32, 512], P('groups', 'ctx')
- decode_out: bfloat16 [2, 32, 512], P('groups', 'ctx')
Inputs may be any that keep to these rules, and one draw needn't show every extreme that they name: `page_table`: row p names the device (column 0, below 32) and the pool slot (column 1, below 16) that take latent page p; no two rows name the same pair.
All inputs are finite; a program needn't handle non-finite values.
Results may differ from a plain program's by a relative error of at most 0.0049.
Values may be sent and summed in bfloat16 or wider, within the bound.
No kernel may reach another device: no remote copies, remote signals or barrier semaphores. Data moves between devices by JAX's collectives and lax.ppermute only.
A program may use at most 64 MiB of HBM per device.

v0:
```python
import functools

import jax
import jax.numpy as jnp
from jax import lax
from jax.experimental import pallas as pl
from jax.experimental.pallas import tpu as pltpu
from jax.sharding import PartitionSpec as P

D_LAT = 512
PAGE = 16
POOL = 16
REQ = 2
LANES = 128

SCALE = 192.0 ** (-0.5)
LOG2E = 1.4426950408889634
NEG = -1e30

VMEM_LIMIT = 8 << 20


def bit_orders(n):
    bits = list(range(n.bit_length() - 2, 0, -1))
    return bits, bits[:-2] + bits[:-3:-1]


def permute_bits(rows, n, even_bit, odd_bit):
    pairs = [(i, i ^ (1 << (odd_bit if i & 1 else even_bit))) for i in range(n)]
    return lax.ppermute(rows, "ctx", pairs)


def decode_kernel(table_ref, lengths_ref, query_ref, cache_ref, latent_ref, packed_ref):
    device = lax.axis_index("ctx")
    rows = latent_ref.shape[0]
    length = cache_ref.shape[2]
    heads = query_ref.shape[1]
    first_page = (device * rows) // PAGE
    token = lax.broadcasted_iota(jnp.int32, (1, rows), 1)
    request = jnp.zeros((1, rows), jnp.int32)
    for k in range(max(1, rows // PAGE)):
        owner = table_ref[0, first_page + k]
        slot = table_ref[1, first_page + k]
        request = jnp.where(token // PAGE == k, lax.rem(owner * POOL + slot, REQ), request)
    position = device * length + lax.broadcasted_iota(jnp.int32, (1, length), 1)
    lane = lax.broadcasted_iota(jnp.int32, (heads, LANES), 1)
    latent = latent_ref[...]
    for r in range(REQ):
        query = query_ref[r]
        cache = cache_ref[r]
        live = position < lengths_ref[r]
        mine = request == r
        cache_scores = jnp.dot(query, cache, preferred_element_type=jnp.float32) * SCALE
        page_scores = (
            lax.dot_general(
                query, latent, (((1,), (1,)), ((), ())), preferred_element_type=jnp.float32
            )
            * SCALE
        )
        top = jnp.maximum(
            jnp.max(jnp.where(live, cache_scores, NEG), axis=1, keepdims=True),
            jnp.max(jnp.where(mine, page_scores, NEG), axis=1, keepdims=True),
        )
        cache_weights = jnp.where(live, jnp.exp(cache_scores - top), 0.0)
        page_weights = jnp.where(mine, jnp.exp(page_scores - top), 0.0)
        total = jnp.sum(cache_weights, axis=1, keepdims=True) + jnp.sum(
            page_weights, axis=1, keepdims=True
        )
        mixed = lax.dot_general(
            cache_weights.astype(jnp.bfloat16),
            cache[:D_LAT],
            (((1,), (1,)), ((), ())),
            preferred_element_type=jnp.float32,
        ) + jnp.dot(
            page_weights.astype(jnp.bfloat16),
            latent[:, :D_LAT],
            preferred_element_type=jnp.float32,
        )
        packed_ref[:, r, :D_LAT] = mixed
        packed_ref[:, r, D_LAT:] = jnp.where(lane == 0, top, total)


def turn_kernel(start, turned_ref, query_ref):
    query_ref[...] = turned_ref[:, start : start + query_ref.shape[0]].T


def turn_query(turned, start, count, params):
    width = turned.shape[0]
    vmem = pl.BlockSpec(memory_space=pltpu.VMEM)
    return pl.pallas_call(
        functools.partial(turn_kernel, start),
        out_shape=jax.ShapeDtypeStruct((count, width), jnp.bfloat16),
        in_specs=[vmem],
        out_specs=vmem,
        compiler_params=params,
        cost_estimate=pl.CostEstimate(
            flops=0, bytes_accessed=4 * count * width, transcendentals=0
        ),
        name="turn_query",
    )(turned)


def place_keys(own_ref, swap_ref, keys, late):
    device = lax.axis_index("ctx")
    parity = lax.rem(device, 2)
    slots, rows, _ = own_ref.shape
    groups = slots // 2
    bits = (groups * 8).bit_length() - 1
    offsets = []
    for side, ref in enumerate((own_ref, swap_ref)):
        odd = parity ^ side
        third = jnp.where(odd == 1, 2, 4)
        fourth = 6 - third
        base = (device & 7) ^ side
        if late:
            base = base ^ fourth
        for half in range(2):
            offsets.append((base ^ third) if half else base)
            place = 2 * side + half
            for t in range(groups):
                mask = 0
                for step in range(bits - 3):
                    if (t >> step) & 1:
                        mask |= 1 << (bits - 4 - step)
                group = (device // 8) ^ mask
                start = pl.multiple_of((group * 4 + place) * rows, rows)
                keys[pl.ds(start, rows)] = ref[half * groups + t]
    column = lax.broadcasted_iota(jnp.int32, (1, 4 * rows), 1)
    token = jnp.zeros((1, 4 * rows), jnp.int32)
    for place, low in enumerate(offsets):
        token = jnp.where(column // rows == place, low * rows + lax.rem(column, rows), token)
    return token


def block_scores(query, keys, token, index, block, columns):
    scores = lax.dot_general(
        query,
        keys[: (index + 1) * columns],
        (((1,), (1,)), ((), ())),
        preferred_element_type=jnp.float32,
    )
    row = lax.broadcasted_iota(jnp.int32, (block, columns), 0)
    diagonal = jnp.where(token <= row, scores[:, index * columns :], NEG)
    if index == 0:
        return diagonal
    return jnp.concatenate([scores[:, : index * columns], diagonal], axis=1)


def early_kernel(most_ref, rest_ref, own_ref, swap_ref, mixed_ref, stats_ref, keys):
    token = place_keys(own_ref, swap_ref, keys, False)
    columns = token.shape[1]
    block = 2 * columns
    lane = lax.broadcasted_iota(jnp.int32, (block, LANES), 1)
    last = most_ref.shape[0] // block
    for index in range(last + 1):
        span = pl.ds(index * block, block)
        query = rest_ref[...] if index == last else most_ref[span]
        scores = block_scores(query, keys, token, index, block, columns)
        top = jnp.max(scores, axis=1, keepdims=True)
        weights = jnp.exp2((scores - top) * (SCALE * LOG2E))
        total = jnp.sum(weights, axis=1, keepdims=True)
        mixed_ref[span] = jnp.dot(
            weights.astype(jnp.bfloat16),
            keys[: (index + 1) * columns, :D_LAT],
            preferred_element_type=jnp.float32,
        )
        stats_ref[span] = jnp.where(lane == 0, top, total)


def late_kernel(
    most_ref,
    rest_ref,
    own_ref,
    swap_ref,
    mixed_ref,
    stats_ref,
    moved_ref,
    out_ref,
    decode_ref,
    keys,
    blocks,
    sems,
):
    token = place_keys(own_ref, swap_ref, keys, True)
    columns = token.shape[1]
    block = 2 * columns
    copies = []
    last = most_ref.shape[0] // block
    for index in range(last + 1):
        span = pl.ds(index * block, block)
        query = rest_ref[...] if index == last else most_ref[span]
        scores = block_scores(query, keys, token, index, block, columns)
        before = stats_ref[span, 0:1]
        top = jnp.maximum(jnp.max(scores, axis=1, keepdims=True), before)
        weights = jnp.exp2((scores - top) * (SCALE * LOG2E))
        factor = jnp.exp2((before - top) * (SCALE * LOG2E))
        total = jnp.sum(weights, axis=1, keepdims=True) + stats_ref[span, 1:2] * factor
        mixed = mixed_ref[span] * factor + jnp.dot(
            weights.astype(jnp.bfloat16),
            keys[: (index + 1) * columns, :D_LAT],
            preferred_element_type=jnp.float32,
        )
        blocks[span] = (mixed / total).astype(jnp.bfloat16)
        copy = pltpu.make_async_copy(blocks.at[span], out_ref.at[span], sems.at[index])
        copy.start()
        copies.append(copy)

    moved = moved_ref[...]
    tops = moved[:, :, D_LAT : D_LAT + 1]
    totals = moved[:, :, D_LAT + 1 : D_LAT + 2]
    scales = jnp.exp(tops - jnp.max(tops, axis=0, keepdims=True))
    own_out = jnp.sum(moved[:, :, :D_LAT] * scales, axis=0)
    decode_ref[...] = (own_out / jnp.sum(totals * scales, axis=0)).astype(jnp.bfloat16)
    for copy in copies:
        copy.wait()


def shards(n, prefill_query, prefill_latent, decode_query, cache, lengths, page_table):
    span = prefill_query.shape[0]
    rows, width = prefill_latent.shape
    heads = decode_query.shape[1]
    vmem = pl.BlockSpec(memory_space=pltpu.VMEM)
    smem = pl.BlockSpec(memory_space=pltpu.SMEM)
    params = pltpu.CompilerParams(vmem_limit_bytes=VMEM_LIMIT)

    even_bits, odd_bits = bit_orders(n)
    held = prefill_latent[None]
    for step, (even, odd) in enumerate(zip(even_bits, odd_bits)):
        received = permute_bits(held, n, even, odd)
        if step < len(even_bits) - 1:
            held = jnp.concatenate([held, received], axis=0)
    held_swap = permute_bits(held, n, 0, 0)
    received_swap = permute_bits(received, n, 0, 0)

    packed = pl.pallas_call(
        decode_kernel,
        out_shape=jax.ShapeDtypeStruct((heads, REQ, D_LAT + LANES), jnp.float32),
        in_specs=[smem, smem, vmem, vmem, vmem],
        out_specs=vmem,
        compiler_params=params,
        cost_estimate=pl.CostEstimate(
            flops=4 * cache.size * heads, bytes_accessed=2 * cache.size, transcendentals=0
        ),
        name="decode_part",
    )(page_table.T, lengths, decode_query, jnp.swapaxes(cache, 1, 2), prefill_latent)
    moved = lax.all_to_all(packed, "ctx", split_axis=0, concat_axis=0, tiled=True)

    turned = jnp.transpose(prefill_query, (1, 2, 0)).reshape(width, span)
    block = 8 * rows
    query_most = turn_query(turned, 0, span - block, params)
    query_rest = turn_query(turned, span - block, block, params)

    cost = pl.CostEstimate(
        flops=2 * span * span * width, bytes_accessed=4 * span * width, transcendentals=0
    )
    keys = pltpu.VMEM((span // 2, width), jnp.bfloat16)
    mixed, stats = pl.pallas_call(
        early_kernel,
        out_shape=(
            jax.ShapeDtypeStruct((span, D_LAT), jnp.float32),
            jax.ShapeDtypeStruct((span, LANES), jnp.float32),
        ),
        in_specs=[vmem] * 4,
        out_specs=(vmem, vmem),
        scratch_shapes=[keys],
        compiler_params=params,
        cost_estimate=cost,
        name="prefill_early",
    )(query_most, query_rest, held, held_swap)
    prefill_out, decode_out = pl.pallas_call(
        late_kernel,
        out_shape=(
            jax.ShapeDtypeStruct((span, D_LAT), jnp.bfloat16),
            jax.ShapeDtypeStruct((REQ, D_LAT), jnp.bfloat16),
        ),
        in_specs=[vmem] * 7,
        out_specs=(pl.BlockSpec(memory_space=pl.ANY), vmem),
        scratch_shapes=[
            keys,
            pltpu.VMEM((span, D_LAT), jnp.bfloat16),
            pltpu.SemaphoreType.DMA((n // 8,)),
        ],
        compiler_params=params,
        cost_estimate=cost,
        name="prefill_late",
    )(query_most, query_rest, received, received_swap, mixed, stats, moved)
    return prefill_out.reshape(span, 1, D_LAT), decode_out.reshape(REQ, 1, D_LAT)


def solution(mesh):
    n = mesh.shape["ctx"]
    in_specs = (
        P("groups", "ctx", None),
        P(("groups", "ctx"), None),
        P("groups", None, None),
        P("groups", "ctx", None),
        P("groups"),
        P("groups", None),
    )
    out_specs = (P("groups", "ctx", None), P("groups", "ctx", None))

    def body(*args):
        return shards(n, *args)

    return jax.shard_map(
        body, mesh=mesh, in_specs=in_specs, out_specs=out_specs, check_vma=False
    )
```

profile of v0, /device:TPU:0, one launch (start us, length us, event | category | flops | bytes accessed | tf_op | source)
XLA Modules:
  0.0 45.9 jit_solution(14660858136345787847)
XLA Ops:
  0.6 0.0 copy-start.4
  0.6 0.0 copy-start.5
  0.7 4.1 %collective-permute-start = (bf16[1,32,576]{2,1,0:T(8,128)(2,1)}, bf16[1,32,576]{2,1,0:T(8,128)(2,1)S(1)}, u32[]{:S(2)}, u32[]{:S(2)}) collective-permute-start(bf16[1,32,576]{2,1,0:T(8,128)(2,1)} %bitcast.11), channel_id=1, source_target_pairs={{0,16},{1,17},{2,18},{3,19},{4,20},{5,21},{6,22},{7,23},{8,24},{9,... | collective-permute-start | bytes 110600 | tf_op jit(solution)/shard_map/ppermute | solution.py:30
  4.8 2.6 %collective-permute-done = bf16[1,32,576]{2,1,0:T(8,128)(2,1)S(1)} collective-permute-done((bf16[1,32,576]{2,1,0:T(8,128)(2,1)}, bf16[1,32,576]{2,1,0:T(8,128)(2,1)S(1)}, u32[]{:S(2)}, u32[]{:S(2)}) %collective-permute-start) | collective-permute-done | bytes 36896 | tf_op jit(solution)/shard_map/ppermute | solution.py:30
  7.4 0.8 %pad_maximum_fusion.2 = bf16[2,32,576]{2,1,0:T(8,128)(2,1)S(1)} fusion(bf16[1,32,576]{2,1,0:T(8,128)(2,1)S(1)} %collective-permute-done, bf16[1,32,576]{2,1,0:T(8,128)(2,1)} %bitcast.12), kind=kLoop, calls=%fused_computation.2 | loop fusion | flops 36864 | bytes 147456 | tf_op jit(solution)/shard_map/concatenate | solution.py:231
  8.2 1.5 %collective-permute-start.1 = (bf16[2,32,576]{2,1,0:T(8,128)(2,1)S(1)}, bf16[2,32,576]{2,1,0:T(8,128)(2,1)S(1)}, u32[]{:S(2)}, u32[]{:S(2)}) collective-permute-start(bf16[2,32,576]{2,1,0:T(8,128)(2,1)S(1)} %pad_maximum_fusion.2), channel_id=1, source_target_pairs={{0,8},{1,9},{2,10},{3,11},{4,12},{5,13},{6,14},{7,15},{8,0},{9,1},... | collective-permute-start | bytes 221192 | tf_op jit(solution)/shard_map/ppermute | solution.py:30
  9.7 3.0 %collective-permute-done.1 = bf16[2,32,576]{2,1,0:T(8,128)(2,1)S(1)} collective-permute-done((bf16[2,32,576]{2,1,0:T(8,128)(2,1)S(1)}, bf16[2,32,576]{2,1,0:T(8,128)(2,1)S(1)}, u32[]{:S(2)}, u32[]{:S(2)}) %collective-permute-start.1) | collective-permute-done | bytes 73760 | tf_op jit(solution)/shard_map/ppermute | solution.py:30
  12.7 0.8 %pad_maximum_fusion.1 = bf16[4,32,576]{2,1,0:T(8,128)(2,1)S(1)} fusion(bf16[2,32,576]{2,1,0:T(8,128)(2,1)S(1)} %collective-permute-done.1, bf16[1,32,576]{2,1,0:T(8,128)(2,1)S(1)} %collective-permute-done, bf16[1,32,576]{2,1,0:T(8,128)(2,1)} %bitcast.13), kind=kLoop, calls=%fused_computation.1 | loop fusion | flops 147456 | bytes 294912 | tf_op jit(solution)/shard_map/concatenate | solution.py:231
  13.5 0.0 copy-start
  13.5 1.8 %collective-permute-start.2 = (bf16[4,32,576]{2,1,0:T(8,128)(2,1)S(1)}, bf16[4,32,576]{2,1,0:T(8,128)(2,1)S(1)}, u32[]{:S(2)}, u32[]{:S(2)}) collective-permute-start(bf16[4,32,576]{2,1,0:T(8,128)(2,1)S(1)} %pad_maximum_fusion.1), channel_id=1, source_target_pairs={{0,4},{1,3},{2,6},{3,1},{4,0},{5,7},{6,2},{7,5},{8,12},{9,11},{10,... | collective-permute-start | bytes 442376 | tf_op jit(solution)/shard_map/ppermute | solution.py:30
  15.3 3.6 %collective-permute-done.2 = bf16[4,32,576]{2,1,0:T(8,128)(2,1)S(1)} collective-permute-done((bf16[4,32,576]{2,1,0:T(8,128)(2,1)S(1)}, bf16[4,32,576]{2,1,0:T(8,128)(2,1)S(1)}, u32[]{:S(2)}, u32[]{:S(2)}) %collective-permute-start.2) | collective-permute-done | bytes 147488 | tf_op jit(solution)/shard_map/ppermute | solution.py:30
  18.9 1.6 %pad_maximum_fusion.own_ref = bf16[8,32,576]{2,1,0:T(8,128)(2,1)} fusion(bf16[4,32,576]{2,1,0:T(8,128)(2,1)S(1)} %collective-permute-done.2, bf16[2,32,576]{2,1,0:T(8,128)(2,1)S(1)} %collective-permute-done.1, bf16[1,32,576]{2,1,0:T(8,128)(2,1)S(1)} %collective-permute-done, bf16[1,32,576]{2,1,0:T(8,128)(2,1)} %bitcast.14), kind=kLoop, calls=%fused_computation | loop fusion | flops 442368 | bytes 589824 | tf_op jit(solution)/shard_map/concatenate | solution.py:231
  20.5 1.7 %collective-permute-start.3 = (bf16[8,32,576]{2,1,0:T(8,128)(2,1)}, bf16[8,32,576]{2,1,0:T(8,128)(2,1)S(1)}, u32[]{:S(2)}, u32[]{:S(2)}) collective-permute-start(bf16[8,32,576]{2,1,0:T(8,128)(2,1)} %pad_maximum_fusion.own_ref), channel_id=1, source_target_pairs={{0,2},{1,5},{2,0},{3,7},{4,6},{5,1},{6,4},{7,3},{8,10},{9,13},{10,... | collective-permute-start | bytes 884744 | tf_op jit(solution)/shard_map/ppermute | solution.py:30
  22.2 0.0 collective-permute-start.5
  22.2 0.0 copy-start.3
  22.2 1.3 %copy-done.3 = bf16[2,512,576]{1,2,0:T(8,128)(2,1)S(1)} copy-done((bf16[2,512,576]{1,2,0:T(8,128)(2,1)S(1)}, bf16[2,512,576]{1,2,0:T(8,128)(2,1)}, u32[]{:S(2)}) %copy-start.3) | copy-done | bytes 1179672
  23.5 0.7 %copy-done.6 = s32[64,2]{0,1:T(2,128)S(1)} copy-done((s32[64,2]{0,1:T(2,128)S(1)}, s32[64,2]{0,1:T(2,128)}, u32[]{:S(2)}) %copy-start.6) | copy-done | bytes 536
  24.1 0.7 %copy-done.7 = s32[2]{0:T(128)S(1)} copy-done((s32[2]{0:T(128)S(1)}, s32[2]{0:T(128)}, u32[]{:S(2)}) %copy-start.7) | copy-done | bytes 32
  24.8 2.1 %decode_part.1 = f32[32,2,640]{2,1,0:T(2,128)} custom-call(s32[2,64]{1,0:T(2,128)S(1)} %bitcast.15, s32[2]{0:T(128)S(1)} %copy-done.7, bf16[2,32,576]{2,1,0:T(8,128)(2,1)S(1)} %copy-done.5, bf16[2,576,512]{2,1,0:T(8,128)(2,1)S(1)} %bitcast.10, bf16[32,576]{1,0:T(8,128)(2,1)S(1)} %copy-done.4), custom_call_target="tpu_custom_call" | custom-call | flops 75497472 | bytes 1179648 | tf_op jit(solution)/shard_map/decode_part/pallas_call | solution.py:235
  26.9 5.0 %all-to-all-start = ((f32[32,2,640]{2,1,0:T(2,128)}), f32[32,2,640]{2,1,0:T(2,128)S(1)}, u32[]{:S(2)}, u32[]{:S(2)}) async-start(f32[32,2,640]{2,1,0:T(2,128)} %decode_part.1), calls=%async_computation | async-start | bytes 327680 | tf_op jit(solution)/shard_map/all_to_all | solution.py:246
  31.9 0.0 collective-permute-done.3.own_ref
  31.9 0.3 collective-permute-start.4
  32.2 0.1 turn_query.3.rest_ref
  32.4 0.3 turn_query.2.most_ref
  32.7 0.0 collective-permute-done.5.swap_ref
  32.7 2.9 %prefill_early.1 = (f32[1024,512]{1,0:T(8,128)S(1)}, f32[1024,128]{1,0:T(8,128)S(1)}) custom-call(bf16[768,576]{1,0:T(8,128)(2,1)S(1)} %turn_query.2.most_ref, bf16[256,576]{1,0:T(8,128)(2,1)S(1)} %turn_query.3.rest_ref, bf16[8,32,576]{2,1,0:T(8,128)(2,1)} %pad_maximum_fusion.own_ref, bf16[8,32,576]{2,1,0:T(8,128)(2,1)} %collective-permute-done.5.swap_ref), custom_call_target="tpu_custom_call" | custom-call | flops 1207959552 | bytes 2359296 | tf_op jit(solution)/shard_map/prefill_early/pallas_call | solution.py:257
  35.6 0.0 copy-start.1
  35.6 1.3 %copy-done.1 = f32[1024,512]{1,0:T(8,128)} copy-done((f32[1024,512]{1,0:T(8,128)}, f32[1024,512]{1,0:T(8,128)S(1)}, u32[]{:S(2)}) %copy-start.1) | copy-done | bytes 2097176
  37.0 3.6 %all-to-all-done.moved_ref = f32[32,2,640]{2,1,0:T(2,128)S(1)} async-done(((f32[32,2,640]{2,1,0:T(2,128)}), f32[32,2,640]{2,1,0:T(2,128)S(1)}, u32[]{:S(2)}, u32[]{:S(2)}) %all-to-all-start) | async-done | bytes 163872 | tf_op jit(solution)/shard_map/all_to_all | solution.py:246
  40.5 0.0 collective-permute-done.4.swap_ref
  40.5 1.6 %copy-done.2 = f32[1024,512]{1,0:T(8,128)S(1)} copy-done((f32[1024,512]{1,0:T(8,128)S(1)}, f32[1024,512]{1,0:T(8,128)}, u32[]{:S(2)}) %copy-start.2) | copy-done | bytes 2097176
  42.1 3.8 %prefill_late.1 = (bf16[1024,512]{1,0:T(8,128)(2,1)}, bf16[2,512]{1,0:T(2,128)(2,1)}) custom-call(bf16[768,576]{1,0:T(8,128)(2,1)S(1)} %turn_query.2.most_ref, bf16[256,576]{1,0:T(8,128)(2,1)S(1)} %turn_query.3.rest_ref, bf16[8,32,576]{2,1,0:T(8,128)(2,1)S(1)} %collective-permute-done.3.own_ref, bf16[8,32,576]{2,1,0:T(8,128)(2,1)S(1)} %collective-permute-done.4.swap_ref, ...), custom_call_target="tpu_custom_call" | custom-call | flops 1207959552 | bytes 2359296 | tf_op jit(solution)/shard_map/prefill_late/pallas_call | solution.py:270
  (6 shorter events, 0.0 us)
Async XLA Ops:
  0.6 21.6 %copy-start.4 = (bf16[32,576]{1,0:T(8,128)(2,1)S(1)}, bf16[32,576]{1,0:T(8,128)(2,1)}, u32[]{:S(2)}) copy-start(bf16[32,576]{1,0:T(8,128)(2,1)} %latent_ref.1) | copy-start | bytes 110596
  0.6 21.6 %copy-start.5 = (bf16[2,32,576]{2,1,0:T(8,128)(2,1)S(1)}, bf16[2,32,576]{2,1,0:T(8,128)(2,1)}, u32[]{:S(2)}) copy-start(bf16[2,32,576]{2,1,0:T(8,128)(2,1)} %query_ref.1) | copy-start | bytes 221188
  0.7 6.8 %collective-permute-start = (bf16[1,32,576]{2,1,0:T(8,128)(2,1)}, bf16[1,32,576]{2,1,0:T(8,128)(2,1)S(1)}, u32[]{:S(2)}, u32[]{:S(2)}) collective-permute-start(bf16[1,32,576]{2,1,0:T(8,128)(2,1)} %bitcast.11), channel_id=1, source_target_pairs={{0,16},{1,17},{2,18},{3,19},{4,20},{5,21},{6,22},{7,23},{8,24},{9,... | collective-permute-start | bytes 110600 | tf_op jit(solution)/shard_map/ppermute | solution.py:30
  8.2 4.5 %collective-permute-start.1 = (bf16[2,32,576]{2,1,0:T(8,128)(2,1)S(1)}, bf16[2,32,576]{2,1,0:T(8,128)(2,1)S(1)}, u32[]{:S(2)}, u32[]{:S(2)}) collective-permute-start(bf16[2,32,576]{2,1,0:T(8,128)(2,1)S(1)} %pad_maximum_fusion.2), channel_id=1, source_target_pairs={{0,8},{1,9},{2,10},{3,11},{4,12},{5,13},{6,14},{7,15},{8,0},{9,1},... | collective-permute-start | bytes 221192 | tf_op jit(solution)/shard_map/ppermute | solution.py:30
  13.5 18.7 %copy-start = (bf16[1024,1,576]{0,2,1:T(8,128)(2,1)S(1)}, bf16[1024,1,576]{0,2,1:T(8,128)(2,1)}, u32[]{:S(2)}) copy-start(bf16[1024,1,576]{0,2,1:T(8,128)(2,1)} %param.6) | copy-start | bytes 3538948
  13.5 5.4 %collective-permute-start.2 = (bf16[4,32,576]{2,1,0:T(8,128)(2,1)S(1)}, bf16[4,32,576]{2,1,0:T(8,128)(2,1)S(1)}, u32[]{:S(2)}, u32[]{:S(2)}) collective-permute-start(bf16[4,32,576]{2,1,0:T(8,128)(2,1)S(1)} %pad_maximum_fusion.1), channel_id=1, source_target_pairs={{0,4},{1,3},{2,6},{3,1},{4,0},{5,7},{6,2},{7,5},{8,12},{9,11},{10,... | collective-permute-start | bytes 442376 | tf_op jit(solution)/shard_map/ppermute | solution.py:30
  20.5 11.4 %collective-permute-start.3 = (bf16[8,32,576]{2,1,0:T(8,128)(2,1)}, bf16[8,32,576]{2,1,0:T(8,128)(2,1)S(1)}, u32[]{:S(2)}, u32[]{:S(2)}) collective-permute-start(bf16[8,32,576]{2,1,0:T(8,128)(2,1)} %pad_maximum_fusion.own_ref), channel_id=1, source_target_pairs={{0,2},{1,5},{2,0},{3,7},{4,6},{5,1},{6,4},{7,3},{8,10},{9,13},{10,... | collective-permute-start | bytes 884744 | tf_op jit(solution)/shard_map/ppermute | solution.py:30
  22.2 10.5 %collective-permute-start.5 = (bf16[8,32,576]{2,1,0:T(8,128)(2,1)}, bf16[8,32,576]{2,1,0:T(8,128)(2,1)}, u32[]{:S(2)}, u32[]{:S(2)}) collective-permute-start(bf16[8,32,576]{2,1,0:T(8,128)(2,1)} %pad_maximum_fusion.own_ref), channel_id=1, source_target_pairs={{0,1},{1,0},{2,3},{3,2},{4,5},{5,4},{6,7},{7,6},{8,9},{9,8},{10,11... | collective-permute-start | bytes 884744 | tf_op jit(solution)/shard_map/ppermute | solution.py:30
  22.2 1.3 %copy-start.3 = (bf16[2,512,576]{1,2,0:T(8,128)(2,1)S(1)}, bf16[2,512,576]{1,2,0:T(8,128)(2,1)}, u32[]{:S(2)}) copy-start(bf16[2,512,576]{1,2,0:T(8,128)(2,1)} %param.9) | copy-start | bytes 3538948
  23.5 0.7 %copy-start.6 = (s32[64,2]{0,1:T(2,128)S(1)}, s32[64,2]{0,1:T(2,128)}, u32[]{:S(2)}) copy-start(s32[64,2]{0,1:T(2,128)} %param.11) | copy-start | bytes 1540
  24.1 0.7 %copy-start.7 = (s32[2]{0:T(128)S(1)}, s32[2]{0:T(128)}, u32[]{:S(2)}) copy-start(s32[2]{0:T(128)} %lengths_ref.1) | copy-start | bytes 28
  26.9 13.7 %all-to-all-start = ((f32[32,2,640]{2,1,0:T(2,128)}), f32[32,2,640]{2,1,0:T(2,128)S(1)}, u32[]{:S(2)}, u32[]{:S(2)}) async-start(f32[32,2,640]{2,1,0:T(2,128)} %decode_part.1), calls=%async_computation | async-start | bytes 327680 | tf_op jit(solution)/shard_map/all_to_all | solution.py:246
  31.9 8.6 %collective-permute-start.4 = (bf16[8,32,576]{2,1,0:T(8,128)(2,1)S(1)}, bf16[8,32,576]{2,1,0:T(8,128)(2,1)S(1)}, u32[]{:S(2)}, u32[]{:S(2)}) collective-permute-start(bf16[8,32,576]{2,1,0:T(8,128)(2,1)S(1)} %collective-permute-done.3.own_ref), channel_id=1, source_target_pairs={{0,1},{1,0},{2,3},{3,2},{4,5},{5,4},{6,7},{7,6},{8,9},{9,8},{10,11... | collective-permute-start | bytes 884744 | tf_op jit(solution)/shard_map/ppermute | solution.py:30
  35.6 1.3 %copy-start.1 = (f32[1024,512]{1,0:T(8,128)}, f32[1024,512]{1,0:T(8,128)S(1)}, u32[]{:S(2)}) copy-start(f32[1024,512]{1,0:T(8,128)S(1)} %get-tuple-element.6.mixed_ref) | copy-start | bytes 6291460
  40.5 1.6 %copy-start.2 = (f32[1024,512]{1,0:T(8,128)S(1)}, f32[1024,512]{1,0:T(8,128)}, u32[]{:S(2)}) copy-start(f32[1024,512]{1,0:T(8,128)} %copy-done.1) | copy-start | bytes 6291460
where the time goes:
time: 46.4 us; the launch traced here: 45.9 us
  starting transfers between devices  14.5 us (31%)
  waiting for transfers between devices  12.8 us (28%)
  Pallas kernels  9.22 us (20%)
  local copies, waits for them, and re-layouts  5.54 us (12%)
  other arithmetic  3.16 us (7%)
  between operations  0.73 us (2%)
    ppermute x6, starting transfers between devices, permute_bits(): return lax.ppermute(rows, 'ctx', pairs)  9.47 us
    ppermute x6, waiting for transfers between devices, permute_bits(): return lax.ppermute(rows, 'ctx', pairs)  9.21 us
    unnamed x16, local copies, waits for them, and re-layouts  5.54 us
    all_to_all x1, starting transfers between devices, shards(): lax.all_to_all(packed, 'ctx', split_axis=0, concat_axis=0, tiled=True)  5.04 us
    pallas_call x1, Pallas kernels, shards(): pl.pallas_call(late_kernel, out_shape=(jax.ShapeDtypeStruct((span, D_LAT)...  3.8 us
    all_to_all x1, waiting for transfers between devices, shards(): lax.all_to_all(packed, 'ctx', split_axis=0, concat_axis=0, tiled=True)  3.56 us
    concatenate x3, other arithmetic, shards(): held = jnp.concatenate([held, received], axis=0)  3.16 us
    pallas_call x1, Pallas kernels, shards(): pl.pallas_call(early_kernel, out_shape=(jax.ShapeDtypeStruct((span, D_LAT...  2.92 us
  transfers between devices with their start and end apart: 7, of which 4 were waited for; matrix products, arithmetic and copies ran while one was open for 0% of the time, Pallas kernels for 12%

commit v1 on v0

--- a/solution.py
+++ b/solution.py
@@ -18,6 +18,7 @@
 NEG = -1e30
 
 VMEM_LIMIT = 8 << 20
+VMEM_MOST = 60 << 20
 
 
 def bit_orders(n):
@@ -30,33 +31,60 @@
     return lax.ppermute(rows, "ctx", pairs)
 
 
-def decode_kernel(table_ref, lengths_ref, query_ref, cache_ref, latent_ref, packed_ref):
+def decode_kernel(
+    table_hbm,
+    lengths_hbm,
+    query_hbm,
+    cache_hbm,
+    latent_hbm,
+    packed_ref,
+    table_ref,
+    lengths_ref,
+    query_ref,
+    cache_ref,
+    latent_ref,
+    sems,
+):
+    moves = [
+        (cache_hbm.at[0], cache_ref.at[0]),
+        (query_hbm, query_ref),
+        (latent_hbm, latent_ref),
+        (table_hbm, table_ref),
+        (lengths_hbm, lengths_ref),
+    ] + [(cache_hbm.at[r], cache_ref.at[r]) for r in range(1, REQ)]
+    copies = [pltpu.make_async_copy(*move, sems.at[i]) for i, move in enumerate(moves)]
+    for copy in copies:
+        copy.start()
+
     device = lax.axis_index("ctx")
     rows = latent_ref.shape[0]
     length = cache_ref.shape[2]
     heads = query_ref.shape[1]
     first_page = (device * rows) // PAGE
     token = lax.broadcasted_iota(jnp.int32, (1, rows), 1)
+    position = device * length + lax.broadcasted_iota(jnp.int32, (1, length), 1)
+    lane = lax.broadcasted_iota(jnp.int32, (heads, LANES), 1)
+    for copy in copies[1:5]:
+        copy.wait()
     request = jnp.zeros((1, rows), jnp.int32)
     for k in range(max(1, rows // PAGE)):
         owner = table_ref[0, first_page + k]
         slot = table_ref[1, first_page + k]
         request = jnp.where(token // PAGE == k, lax.rem(owner * POOL + slot, REQ), request)
-    position = device * length + lax.broadcasted_iota(jnp.int32, (1, length), 1)
-    lane = lax.broadcasted_iota(jnp.int32, (heads, LANES), 1)
     latent = latent_ref[...]
     for r in range(REQ):
         query = query_ref[r]
-        cache = cache_ref[r]
         live = position < lengths_ref[r]
         mine = request == r
-        cache_scores = jnp.dot(query, cache, preferred_element_type=jnp.float32) * SCALE
         page_scores = (
             lax.dot_general(
                 query, latent, (((1,), (1,)), ((), ())), preferred_element_type=jnp.float32
             )
             * SCALE
         )
+        copies[0 if r == 0 else 4 + r].wait()
+        cache = cache_ref[r]
+        cache_scores = jnp.dot(query, cache, preferred_element_type=jnp.float32) * SCALE
         top = jnp.maximum(
             jnp.max(jnp.where(live, cache_scores, NEG), axis=1, keepdims=True),
             jnp.max(jnp.where(mine, page_scores, NEG), axis=1, keepdims=True),
@@ -78,6 +106,15 @@
         )
         packed_ref[:, r, :D_LAT] = mixed
         packed_ref[:, r, D_LAT:] = jnp.where(lane == 0, top, total)
+
+
+def merge_kernel(moved_ref, decode_ref):
+    moved = moved_ref[...]
+    tops = moved[:, :, D_LAT : D_LAT + 1]
+    totals = moved[:, :, D_LAT + 1 : D_LAT + 2]
+    scales = jnp.exp(tops - jnp.max(tops, axis=0, keepdims=True))
+    own_out = jnp.sum(moved[:, :, :D_LAT] * scales, axis=0)
+    decode_ref[...] = (own_out / jnp.sum(totals * scales, axis=0)).astype(jnp.bfloat16)
 
 
 def turn_kernel(start, turned_ref, query_ref):
@@ -146,13 +183,16 @@
     return jnp.concatenate([scores[:, : index * columns], diagonal], axis=1)
 
 
-def early_kernel(most_ref, rest_ref, own_ref, swap_ref, mixed_ref, stats_ref, keys):
+def early_kernel(
+    most_ref, rest_ref, own_ref, swap_ref, mixed_hbm, stats_ref, keys, mixed_ref, sems
+):
     token = place_keys(own_ref, swap_ref, keys, False)
     columns = token.shape[1]
     block = 2 * columns
     lane = lax.broadcasted_iota(jnp.int32, (block, LANES), 1)
     last = most_ref.shape[0] // block
-    for index in range(last + 1):
+    copies = []
+    for index in range(last, -1, -1):
         span = pl.ds(index * block, block)
         query = rest_ref[...] if index == last else most_ref[span]
         scores = block_scores(query, keys, token, index, block, columns)
@@ -165,6 +205,11 @@
             preferred_element_type=jnp.float32,
         )
         stats_ref[span] = jnp.where(lane == 0, top, total)
+        copy = pltpu.make_async_copy(mixed_ref.at[span], mixed_hbm.at[span], sems.at[index])
+        copy.start()
+        copies.append(copy)
+    for copy in copies:
+        copy.wait()
 
 
 def late_kernel(
@@ -172,22 +217,29 @@
     rest_ref,
     own_ref,
     swap_ref,
+    mixed_hbm,
+    stats_ref,
+    out_ref,
+    keys,
     mixed_ref,
-    stats_ref,
-    moved_ref,
-    out_ref,
-    decode_ref,
-    keys,
     blocks,
-    sems,
+    in_sems,
+    out_sems,
 ):
+    columns = 4 * own_ref.shape[1]
+    block = 2 * columns
+    last = most_ref.shape[0] // block
+    spans = [pl.ds(index * block, block) for index in range(last + 1)]
+    loads = [
+        pltpu.make_async_copy(mixed_hbm.at[span], mixed_ref.at[span], in_sems.at[index])
+        for index, span in enumerate(spans)
+    ]
+    for load in loads[::-1]:
+        load.start()
     token = place_keys(own_ref, swap_ref, keys, True)
-    columns = token.shape[1]
-    block = 2 * columns
-    copies = []
-    last = most_ref.shape[0] // block
-    for index in range(last + 1):
-        span = pl.ds(index * block, block)
+    stores = []
+    for index in range(last, -1, -1):
+        span = spans[index]
         query = rest_ref[...] if index == last else most_ref[span]
         scores = block_scores(query, keys, token, index, block, columns)
         before = stats_ref[span, 0:1]
@@ -195,24 +247,19 @@
         weights = jnp.exp2((scores - top) * (SCALE * LOG2E))
         factor = jnp.exp2((before - top) * (SCALE * LOG2E))
         total = jnp.sum(weights, axis=1, keepdims=True) + stats_ref[span, 1:2] * factor
-        mixed = mixed_ref[span] * factor + jnp.dot(
+        mixed = jnp.dot(
             weights.astype(jnp.bfloat16),
             keys[: (index + 1) * columns, :D_LAT],
             preferred_element_type=jnp.float32,
         )
-        blocks[span] = (mixed / total).astype(jnp.bfloat16)
-        copy = pltpu.make_async_copy(blocks.at[span], out_ref.at[span], sems.at[index])
-        copy.start()
-        copies.append(copy)
-
-    moved = moved_ref[...]
-    tops = moved[:, :, D_LAT : D_LAT + 1]
-    totals = moved[:, :, D_LAT + 1 : D_LAT + 2]
-    scales = jnp.exp(tops - jnp.max(tops, axis=0, keepdims=True))
-    own_out = jnp.sum(moved[:, :, :D_LAT] * scales, axis=0)
-    decode_ref[...] = (own_out / jnp.sum(totals * scales, axis=0)).astype(jnp.bfloat16)
-    for copy in copies:
-        copy.wait()
+        scale = 1.0 / total
+        loads[index].wait()
+        blocks[span] = (mixed_ref[span] * (factor * scale) + mixed * scale).astype(jnp.bfloat16)
+        store = pltpu.make_async_copy(blocks.at[span], out_ref.at[span], out_sems.at[index])
+        store.start()
+        stores.append(store)
+    for store in stores:
+        store.wait()
 
 
 def shards(n, prefill_query, prefill_latent, decode_query, cache, lengths, page_table):
@@ -220,7 +267,7 @@
     rows, width = prefill_latent.shape
     heads = decode_query.shape[1]
     vmem = pl.BlockSpec(memory_space=pltpu.VMEM)
-    smem = pl.BlockSpec(memory_space=pltpu.SMEM)
+    hbm = pl.BlockSpec(memory_space=pltpu.HBM)
     params = pltpu.CompilerParams(vmem_limit_bytes=VMEM_LIMIT)
 
     even_bits, odd_bits = bit_orders(n)
@@ -235,9 +282,17 @@
     packed = pl.pallas_call(
         decode_kernel,
         out_shape=jax.ShapeDtypeStruct((heads, REQ, D_LAT + LANES), jnp.float32),
-        in_specs=[smem, smem, vmem, vmem, vmem],
+        in_specs=[hbm] * 5,
         out_specs=vmem,
-        compiler_params=params,
+        scratch_shapes=[
+            pltpu.SMEM(page_table.shape[::-1], jnp.int32),
+            pltpu.SMEM(lengths.shape, jnp.int32),
+            pltpu.VMEM(decode_query.shape, jnp.bfloat16),
+            pltpu.VMEM((REQ, width, cache.shape[1]), jnp.bfloat16),
+            pltpu.VMEM((rows, width), jnp.bfloat16),
+            pltpu.SemaphoreType.DMA((4 + REQ,)),
+        ],
+        compiler_params=pltpu.CompilerParams(vmem_limit_bytes=VMEM_MOST),
         cost_estimate=pl.CostEstimate(
             flops=4 * cache.size * heads, bytes_accessed=2 * cache.size, transcendentals=0
         ),
@@ -254,36 +309,40 @@
         flops=2 * span * span * width, bytes_accessed=4 * span * width, transcendentals=0
     )
     keys = pltpu.VMEM((span // 2, width), jnp.bfloat16)
+    sums = pltpu.VMEM((span, D_LAT), jnp.float32)
+    sems = pltpu.SemaphoreType.DMA((n // 8,))
     mixed, stats = pl.pallas_call(
         early_kernel,
         out_shape=(
-            jax.ShapeDtypeStruct((span, D_LAT), jnp.float32),
+            pltpu.HBM((span, D_LAT), jnp.float32),
             jax.ShapeDtypeStruct((span, LANES), jnp.float32),
         ),
         in_specs=[vmem] * 4,
-        out_specs=(vmem, vmem),
-        scratch_shapes=[keys],
+        out_specs=(hbm, vmem),
+        scratch_shapes=[keys, sums, sems],
         compiler_params=params,
         cost_estimate=cost,
         name="prefill_early",
     )(query_most, query_rest, held, held_swap)
-    prefill_out, decode_out = pl.pallas_call(
+    decode_out = pl.pallas_call(
+        merge_kernel,
+        out_shape=jax.ShapeDtypeStruct((REQ, D_LAT), jnp.bfloat16),
+        in_specs=[vmem],
+        out_specs=vmem,
+        compiler_params=params,
+        cost_estimate=pl.CostEstimate(flops=moved.size, bytes_accessed=16, transcendentals=0),
+        name="decode_merge",
+    )(moved)
+    prefill_out = pl.pallas_call(
         late_kernel,
-        out_shape=(
-            jax.ShapeDtypeStruct((span, D_LAT), jnp.bfloat16),
-            jax.ShapeDtypeStruct((REQ, D_LAT), jnp.bfloat16),
-        ),
-        in_specs=[vmem] * 7,
-        out_specs=(pl.BlockSpec(memory_space=pl.ANY), vmem),
-        scratch_shapes=[
-            keys,
-            pltpu.VMEM((span, D_LAT), jnp.bfloat16),
-            pltpu.SemaphoreType.DMA((n // 8,)),
-        ],
+        out_shape=jax.ShapeDtypeStruct((span, D_LAT), jnp.bfloat16),
+        in_specs=[vmem] * 4 + [hbm, vmem],
+        out_specs=hbm,
+        scratch_shapes=[keys, sums, pltpu.VMEM((span, D_LAT), jnp.bfloat16), sems, sems],
         compiler_params=params,
         cost_estimate=cost,
         name="prefill_late",
-    )(query_most, query_rest, received, received_swap, mixed, stats, moved)
+    )(query_most, query_rest, received, received_swap, mixed, stats)
     return prefill_out.reshape(span, 1, D_LAT), decode_out.reshape(REQ, 1, D_LAT)
 
 

time: 46.4 us -> 50.2 us (1.082)
  waiting for transfers between devices: 12.8 us -> 16.8 us
  local copies, waits for them, and re-layouts: 5.54 us -> 1.59 us
  Pallas kernels: 9.22 us -> 12.9 us
    all_to_all x1, waiting for transfers between devices: 3.56 us -> 7.59 us  [shards(): lax.all_to_all(packed, 'ctx', split_axis=0, concat_axis=0, tiled=True)]
    unnamed x16 -> x4, local copies, waits for them, and re-layouts: 5.54 us -> 1.59 us
    pallas_call x2 -> x3, Pallas kernels: 6.72 us -> 9.34 us  [the longest x1 4.45 us: shards(): pl.pallas_call(late_kernel, out_shape=jax.ShapeDtypeStruct((span, D_LAT),...]
    pallas_call x1, Pallas kernels: 2.06 us -> 3.12 us  [shards(): pl.pallas_call(decode_kernel, out_shape=jax.ShapeDtypeStruct((heads, REQ,...]
  transfers between devices with their start and end apart: 7 -> 7, of which waited for: 4 -> 4; matrix products, arithmetic and copies ran while one was open for 0% -> 0% of each run, Pallas kernels for 12% -> 17%
where the time goes in v1:
time: 50.2 us; the launch traced here: 49.8 us
  waiting for transfers between devices  16.8 us (33%)
  starting transfers between devices  14.7 us (29%)
  Pallas kernels  12.9 us (26%)
  other arithmetic  3.16 us (6%)
  local copies, waits for them, and re-layouts  1.59 us (3%)
  between operations  0.7 us (1%)
    ppermute x6, starting transfers between devices, permute_bits(): return lax.ppermute(rows, 'ctx', pairs)  9.72 us
    ppermute x6, waiting for transfers between devices, permute_bits(): return lax.ppermute(rows, 'ctx', pairs)  9.21 us
    all_to_all x1, waiting for transfers between devices, shards(): lax.all_to_all(packed, 'ctx', split_axis=0, concat_axis=0, tiled=True)  7.59 us
    all_to_all x1, starting transfers between devices, shards(): lax.all_to_all(packed, 'ctx', split_axis=0, concat_axis=0, tiled=True)  4.94 us
    pallas_call x1, Pallas kernels, shards(): pl.pallas_call(late_kernel, out_shape=jax.ShapeDtypeStruct((span, D_LAT),...  4.45 us
    pallas_call x1, Pallas kernels, shards(): pl.pallas_call(early_kernel, out_shape=(pltpu.HBM((span, D_LAT), jnp.floa...  4.1 us
    concatenate x3, other arithmetic, shards(): held = jnp.concatenate([held, received], axis=0)  3.16 us
    pallas_call x1, Pallas kernels, shards(): pl.pallas_call(decode_kernel, out_shape=jax.ShapeDtypeStruct((heads, REQ,...  3.12 us
  transfers between devices with their start and end apart: 7, of which 4 were waited for; matrix products, arithmetic and copies ran while one was open for 0% of the time, Pallas kernels for 17%

profile of v1, /device:TPU:0, one launch (start us, length us, event | category | flops | bytes accessed | tf_op | source)
XLA Modules:
  0.0 49.8 jit_solution(15225570011505244135)
XLA Ops:
  0.6 4.1 %collective-permute-start = (bf16[1,32,576]{2,1,0:T(8,128)(2,1)}, bf16[1,32,576]{2,1,0:T(8,128)(2,1)S(1)}, u32[]{:S(2)}, u32[]{:S(2)}) collective-permute-start(bf16[1,32,576]{2,1,0:T(8,128)(2,1)} %bitcast.12), channel_id=1, source_target_pairs={{0,16},{1,17},{2,18},{3,19},{4,20},{5,21},{6,22},{7,23},{8,24},{9,... | collective-permute-start | bytes 110600 | tf_op jit(solution)/shard_map/ppermute | solution.py:31
  4.8 2.6 %collective-permute-done = bf16[1,32,576]{2,1,0:T(8,128)(2,1)S(1)} collective-permute-done((bf16[1,32,576]{2,1,0:T(8,128)(2,1)}, bf16[1,32,576]{2,1,0:T(8,128)(2,1)S(1)}, u32[]{:S(2)}, u32[]{:S(2)}) %collective-permute-start) | collective-permute-done | bytes 36896 | tf_op jit(solution)/shard_map/ppermute | solution.py:31
  7.4 0.8 %pad_maximum_fusion.2 = bf16[2,32,576]{2,1,0:T(8,128)(2,1)S(1)} fusion(bf16[1,32,576]{2,1,0:T(8,128)(2,1)S(1)} %collective-permute-done, bf16[1,32,576]{2,1,0:T(8,128)(2,1)} %bitcast.13), kind=kLoop, calls=%fused_computation.2 | loop fusion | flops 36864 | bytes 147456 | tf_op jit(solution)/shard_map/concatenate | solution.py:278
  8.2 1.5 %collective-permute-start.1 = (bf16[2,32,576]{2,1,0:T(8,128)(2,1)S(1)}, bf16[2,32,576]{2,1,0:T(8,128)(2,1)S(1)}, u32[]{:S(2)}, u32[]{:S(2)}) collective-permute-start(bf16[2,32,576]{2,1,0:T(8,128)(2,1)S(1)} %pad_maximum_fusion.2), channel_id=1, source_target_pairs={{0,8},{1,9},{2,10},{3,11},{4,12},{5,13},{6,14},{7,15},{8,0},{9,1},... | collective-permute-start | bytes 221192 | tf_op jit(solution)/shard_map/ppermute | solution.py:31
  9.7 3.0 %collective-permute-done.1 = bf16[2,32,576]{2,1,0:T(8,128)(2,1)S(1)} collective-permute-done((bf16[2,32,576]{2,1,0:T(8,128)(2,1)S(1)}, bf16[2,32,576]{2,1,0:T(8,128)(2,1)S(1)}, u32[]{:S(2)}, u32[]{:S(2)}) %collective-permute-start.1) | collective-permute-done | bytes 73760 | tf_op jit(solution)/shard_map/ppermute | solution.py:31
  12.7 0.8 %pad_maximum_fusion.1 = bf16[4,32,576]{2,1,0:T(8,128)(2,1)S(1)} fusion(bf16[2,32,576]{2,1,0:T(8,128)(2,1)S(1)} %collective-permute-done.1, bf16[1,32,576]{2,1,0:T(8,128)(2,1)S(1)} %collective-permute-done, bf16[1,32,576]{2,1,0:T(8,128)(2,1)} %bitcast.14), kind=kLoop, calls=%fused_computation.1 | loop fusion | flops 147456 | bytes 294912 | tf_op jit(solution)/shard_map/concatenate | solution.py:278
  13.5 0.0 copy-start
  13.5 1.8 %collective-permute-start.2 = (bf16[4,32,576]{2,1,0:T(8,128)(2,1)S(1)}, bf16[4,32,576]{2,1,0:T(8,128)(2,1)S(1)}, u32[]{:S(2)}, u32[]{:S(2)}) collective-permute-start(bf16[4,32,576]{2,1,0:T(8,128)(2,1)S(1)} %pad_maximum_fusion.1), channel_id=1, source_target_pairs={{0,4},{1,3},{2,6},{3,1},{4,0},{5,7},{6,2},{7,5},{8,12},{9,11},{10,... | collective-permute-start | bytes 442376 | tf_op jit(solution)/shard_map/ppermute | solution.py:31
  15.3 3.6 %collective-permute-done.2 = bf16[4,32,576]{2,1,0:T(8,128)(2,1)S(1)} collective-permute-done((bf16[4,32,576]{2,1,0:T(8,128)(2,1)S(1)}, bf16[4,32,576]{2,1,0:T(8,128)(2,1)S(1)}, u32[]{:S(2)}, u32[]{:S(2)}) %collective-permute-start.2) | collective-permute-done | bytes 147488 | tf_op jit(solution)/shard_map/ppermute | solution.py:31
  18.9 1.6 %pad_maximum_fusion.own_ref = bf16[8,32,576]{2,1,0:T(8,128)(2,1)} fusion(bf16[4,32,576]{2,1,0:T(8,128)(2,1)S(1)} %collective-permute-done.2, bf16[2,32,576]{2,1,0:T(8,128)(2,1)S(1)} %collective-permute-done.1, bf16[1,32,576]{2,1,0:T(8,128)(2,1)S(1)} %collective-permute-done, bf16[1,32,576]{2,1,0:T(8,128)(2,1)} %bitcast.15), kind=kLoop, calls=%fused_computation | loop fusion | flops 442368 | bytes 589824 | tf_op jit(solution)/shard_map/concatenate | solution.py:278
  20.5 1.7 %collective-permute-start.3 = (bf16[8,32,576]{2,1,0:T(8,128)(2,1)}, bf16[8,32,576]{2,1,0:T(8,128)(2,1)S(1)}, u32[]{:S(2)}, u32[]{:S(2)}) collective-permute-start(bf16[8,32,576]{2,1,0:T(8,128)(2,1)} %pad_maximum_fusion.own_ref), channel_id=1, source_target_pairs={{0,2},{1,5},{2,0},{3,7},{4,6},{5,1},{6,4},{7,3},{8,10},{9,13},{10,... | collective-permute-start | bytes 884744 | tf_op jit(solution)/shard_map/ppermute | solution.py:31
  22.2 3.1 %decode_part.1 = f32[32,2,640]{2,1,0:T(2,128)} custom-call(s32[2,64]{1,0:T(2,128)} %bitcast.17, s32[2]{0:T(128)} %lengths_hbm.1, bf16[2,32,576]{2,1,0:T(8,128)(2,1)} %query_hbm.1, bf16[2,576,512]{2,1,0:T(8,128)(2,1)} %bitcast.10, bf16[32,576]{1,0:T(8,128)(2,1)} %latent_hbm.1), custom_call_target="tpu_custom_call" | custom-call | flops 75497472 | bytes 1179648 | tf_op jit(solution)/shard_map/decode_part/pallas_call | solution.py:282
  25.3 4.9 %all-to-all-start = ((f32[32,2,640]{2,1,0:T(2,128)}), f32[32,2,640]{2,1,0:T(2,128)S(1)}, u32[]{:S(2)}, u32[]{:S(2)}) async-start(f32[32,2,640]{2,1,0:T(2,128)} %decode_part.1), calls=%async_computation | async-start | bytes 327680 | tf_op jit(solution)/shard_map/all_to_all | solution.py:301
  30.2 0.3 collective-permute-start.5
  30.6 0.0 collective-permute-done.3.own_ref
  30.6 0.3 collective-permute-start.4
  30.8 0.0 copy-done
  30.8 0.3 turn_query.2.most_ref
  31.1 0.1 turn_query.3.rest_ref
  31.3 7.6 %all-to-all-done.moved_ref = f32[32,2,640]{2,1,0:T(2,128)S(1)} async-done(((f32[32,2,640]{2,1,0:T(2,128)}), f32[32,2,640]{2,1,0:T(2,128)S(1)}, u32[]{:S(2)}, u32[]{:S(2)}) %all-to-all-start) | async-done | bytes 163872 | tf_op jit(solution)/shard_map/all_to_all | solution.py:301
  38.9 0.8 %decode_merge.1 = bf16[2,512]{1,0:T(2,128)(2,1)} custom-call(f32[32,2,640]{2,1,0:T(2,128)S(1)} %all-to-all-done.moved_ref), custom_call_target="tpu_custom_call" | custom-call | flops 40960 | bytes 16 | tf_op jit(solution)/shard_map/decode_merge/pallas_call | solution.py:327
  39.6 0.0 collective-permute-done.5.swap_ref
  39.6 4.1 %prefill_early.1 = (f32[1024,512]{1,0:T(8,128)}, f32[1024,128]{1,0:T(8,128)S(1)}) custom-call(bf16[768,576]{1,0:T(8,128)(2,1)S(1)} %turn_query.2.most_ref, bf16[256,576]{1,0:T(8,128)(2,1)S(1)} %turn_query.3.rest_ref, bf16[8,32,576]{2,1,0:T(8,128)(2,1)} %pad_maximum_fusion.own_ref, bf16[8,32,576]{2,1,0:T(8,128)(2,1)} %collective-permute-done.5.swap_ref), custom_call_target="tpu_custom_call" | custom-call | flops 1207959552 | bytes 2359296 | tf_op jit(solution)/shard_map/prefill_early/pallas_call | solution.py:314
  43.8 0.0 collective-permute-done.4.swap_ref
  43.8 0.0 copy-start.1
  43.8 1.6 %copy-done.1 = f32[1024,512]{1,0:T(8,128)S(1)} copy-done((f32[1024,512]{1,0:T(8,128)S(1)}, f32[1024,512]{1,0:T(8,128)}, u32[]{:S(2)}) %copy-start.1) | copy-done | bytes 2097176
  45.4 4.5 %prefill_late.1 = bf16[1024,512]{1,0:T(8,128)(2,1)} custom-call(bf16[768,576]{1,0:T(8,128)(2,1)S(1)} %turn_query.2.most_ref, bf16[256,576]{1,0:T(8,128)(2,1)S(1)} %turn_query.3.rest_ref, bf16[8,32,576]{2,1,0:T(8,128)(2,1)S(1)} %collective-permute-done.3.own_ref, bf16[8,32,576]{2,1,0:T(8,128)(2,1)S(1)} %collective-permute-done.4.swap_ref, ...), custom_call_target="tpu_custom_call" | custom-call | flops 1207959552 | bytes 2359296 | tf_op jit(solution)/shard_map/prefill_late/pallas_call | solution.py:336
Async XLA Ops:
  0.6 6.8 %collective-permute-start = (bf16[1,32,576]{2,1,0:T(8,128)(2,1)}, bf16[1,32,576]{2,1,0:T(8,128)(2,1)S(1)}, u32[]{:S(2)}, u32[]{:S(2)}) collective-permute-start(bf16[1,32,576]{2,1,0:T(8,128)(2,1)} %bitcast.12), channel_id=1, source_target_pairs={{0,16},{1,17},{2,18},{3,19},{4,20},{5,21},{6,22},{7,23},{8,24},{9,... | collective-permute-start | bytes 110600 | tf_op jit(solution)/shard_map/ppermute | solution.py:31
  8.2 4.5 %collective-permute-start.1 = (bf16[2,32,576]{2,1,0:T(8,128)(2,1)S(1)}, bf16[2,32,576]{2,1,0:T(8,128)(2,1)S(1)}, u32[]{:S(2)}, u32[]{:S(2)}) collective-permute-start(bf16[2,32,576]{2,1,0:T(8,128)(2,1)S(1)} %pad_maximum_fusion.2), channel_id=1, source_target_pairs={{0,8},{1,9},{2,10},{3,11},{4,12},{5,13},{6,14},{7,15},{8,0},{9,1},... | collective-permute-start | bytes 221192 | tf_op jit(solution)/shard_map/ppermute | solution.py:31
  13.5 17.3 %copy-start = (bf16[1024,1,576]{0,2,1:T(8,128)(2,1)S(1)}, bf16[1024,1,576]{0,2,1:T(8,128)(2,1)}, u32[]{:S(2)}) copy-start(bf16[1024,1,576]{0,2,1:T(8,128)(2,1)} %param.6) | copy-start | bytes 3538948
  13.5 5.4 %collective-permute-start.2 = (bf16[4,32,576]{2,1,0:T(8,128)(2,1)S(1)}, bf16[4,32,576]{2,1,0:T(8,128)(2,1)S(1)}, u32[]{:S(2)}, u32[]{:S(2)}) collective-permute-start(bf16[4,32,576]{2,1,0:T(8,128)(2,1)S(1)} %pad_maximum_fusion.1), channel_id=1, source_target_pairs={{0,4},{1,3},{2,6},{3,1},{4,0},{5,7},{6,2},{7,5},{8,12},{9,11},{10,... | collective-permute-start | bytes 442376 | tf_op jit(solution)/shard_map/ppermute | solution.py:31
  20.5 10.1 %collective-permute-start.3 = (bf16[8,32,576]{2,1,0:T(8,128)(2,1)}, bf16[8,32,576]{2,1,0:T(8,128)(2,1)S(1)}, u32[]{:S(2)}, u32[]{:S(2)}) collective-permute-start(bf16[8,32,576]{2,1,0:T(8,128)(2,1)} %pad_maximum_fusion.own_ref), channel_id=1, source_target_pairs={{0,2},{1,5},{2,0},{3,7},{4,6},{5,1},{6,4},{7,3},{8,10},{9,13},{10,... | collective-permute-start | bytes 884744 | tf_op jit(solution)/shard_map/ppermute | solution.py:31
  25.3 13.6 %all-to-all-start = ((f32[32,2,640]{2,1,0:T(2,128)}), f32[32,2,640]{2,1,0:T(2,128)S(1)}, u32[]{:S(2)}, u32[]{:S(2)}) async-start(f32[32,2,640]{2,1,0:T(2,128)} %decode_part.1), calls=%async_computation | async-start | bytes 327680 | tf_op jit(solution)/shard_map/all_to_all | solution.py:301
  30.2 9.4 %collective-permute-start.5 = (bf16[8,32,576]{2,1,0:T(8,128)(2,1)}, bf16[8,32,576]{2,1,0:T(8,128)(2,1)}, u32[]{:S(2)}, u32[]{:S(2)}) collective-permute-start(bf16[8,32,576]{2,1,0:T(8,128)(2,1)} %pad_maximum_fusion.own_ref), channel_id=1, source_target_pairs={{0,1},{1,0},{2,3},{3,2},{4,5},{5,4},{6,7},{7,6},{8,9},{9,8},{10,11... | collective-permute-start | bytes 884744 | tf_op jit(solution)/shard_map/ppermute | solution.py:31
  30.6 13.2 %collective-permute-start.4 = (bf16[8,32,576]{2,1,0:T(8,128)(2,1)S(1)}, bf16[8,32,576]{2,1,0:T(8,128)(2,1)S(1)}, u32[]{:S(2)}, u32[]{:S(2)}) collective-permute-start(bf16[8,32,576]{2,1,0:T(8,128)(2,1)S(1)} %collective-permute-done.3.own_ref), channel_id=1, source_target_pairs={{0,1},{1,0},{2,3},{3,2},{4,5},{5,4},{6,7},{7,6},{8,9},{9,8},{10,11... | collective-permute-start | bytes 884744 | tf_op jit(solution)/shard_map/ppermute | solution.py:31
  43.8 1.6 %copy-start.1 = (f32[1024,512]{1,0:T(8,128)S(1)}, f32[1024,512]{1,0:T(8,128)}, u32[]{:S(2)}) copy-start(f32[1024,512]{1,0:T(8,128)} %get-tuple-element.4.mixed_hbm) | copy-start | bytes 6291460

commit v2 on v1

v2 whole, which is shorter than its diff:
```python
import functools

import jax
import jax.numpy as jnp
from jax import lax
from jax.experimental import pallas as pl
from jax.experimental.pallas import tpu as pltpu
from jax.sharding import PartitionSpec as P

D_LAT = 512
PAGE = 16
POOL = 16
REQ = 2
LANES = 128
GROUP = D_LAT // LANES

SCALE = 192.0 ** (-0.5)
LOG2E = 1.4426950408889634
NEG = -1e30
SOFTMAX_ROWS = 64

VMEM_LIMIT = 8 << 20
VMEM_MOST = 60 << 20


def bit_orders(n):
    bits = list(range(n.bit_length() - 2, 0, -1))
    return bits, bits[-1:] + bits[:-1]


def permute_bits(rows, n, even_bit, odd_bit):
    pairs = [(i, i ^ (1 << (odd_bit if i & 1 else even_bit))) for i in range(n)]
    return lax.ppermute(rows, "ctx", pairs)


def split_parts(value):
    parts = []
    for _ in range(3):
        part = value.astype(jnp.bfloat16).astype(jnp.float32)
        parts.append(part)
        value = value - part
    return parts


def pack_stats(top, total, lane):
    stats = jnp.zeros((top.shape[0], LANES), jnp.float32)
    for k, part in enumerate(split_parts(top) + split_parts(total)):
        stats = jnp.where(lane == k, part, stats)
    return stats


def spread_stats(packed):
    source = lax.broadcasted_iota(jnp.int32, (LANES, 2 * LANES), 0)
    target = lax.broadcasted_iota(jnp.int32, (LANES, 2 * LANES), 1)
    ones = jnp.where(source // 3 == target // LANES, 1.0, 0.0).astype(jnp.bfloat16)
    return jnp.dot(packed, ones, preferred_element_type=jnp.float32)


def decode_kernel(
    table_hbm,
    lengths_hbm,
    query_hbm,
    cache_hbm,
    latent_hbm,
    packed_ref,
    table_ref,
    lengths_ref,
    query_ref,
    cache_ref,
    latent_ref,
    rows_ref,
    sems,
):
    moves = [
        (cache_hbm.at[0], cache_ref.at[0]),
        (query_hbm, query_ref),
        (latent_hbm, latent_ref),
        (table_hbm, table_ref),
        (lengths_hbm, lengths_ref),
    ] + [(cache_hbm.at[r], cache_ref.at[r]) for r in range(1, REQ)]
    copies = [pltpu.make_async_copy(*move, sems.at[i]) for i, move in enumerate(moves)]
    for copy in copies:
        copy.start()

    device = lax.axis_index("ctx")
    rows = latent_ref.shape[0]
    length = cache_ref.shape[2]
    heads = query_ref.shape[1]
    first_page = (device * rows) // PAGE
    token = lax.broadcasted_iota(jnp.int32, (1, rows), 1)
    position = device * length + lax.broadcasted_iota(jnp.int32, (1, length), 1)
    lane = lax.broadcasted_iota(jnp.int32, (heads, LANES), 1)
    for copy in copies[1:5]:
        copy.wait()
    request = jnp.zeros((1, rows), jnp.int32)
    for k in range(max(1, rows // PAGE)):
        owner = table_ref[0, first_page + k]
        slot = table_ref[1, first_page + k]
        request = jnp.where(token // PAGE == k, lax.rem(owner * POOL + slot, REQ), request)
    latent = latent_ref[...]
    for r in range(REQ):
        query = query_ref[r]
        live = position < lengths_ref[r]
        mine = request == r
        page_scores = (
            lax.dot_general(
                query, latent, (((1,), (1,)), ((), ())), preferred_element_type=jnp.float32
            )
            * SCALE
        )
        copies[0 if r == 0 else 4 + r].wait()
        cache = cache_ref[r]
        cache_scores = jnp.dot(query, cache, preferred_element_type=jnp.float32) * SCALE
        top = jnp.maximum(
            jnp.max(jnp.where(live, cache_scores, NEG), axis=1, keepdims=True),
            jnp.max(jnp.where(mine, page_scores, NEG), axis=1, keepdims=True),
        )
        cache_weights = jnp.where(live, jnp.exp(cache_scores - top), 0.0)
        page_weights = jnp.where(mine, jnp.exp(page_scores - top), 0.0)
        total = jnp.sum(cache_weights, axis=1, keepdims=True) + jnp.sum(
            page_weights, axis=1, keepdims=True
        )
        mixed = lax.dot_general(
            cache_weights.astype(jnp.bfloat16),
            cache[:D_LAT],
            (((1,), (1,)), ((), ())),
            preferred_element_type=jnp.float32,
        ) + jnp.dot(
            page_weights.astype(jnp.bfloat16),
            latent[:, :D_LAT],
            preferred_element_type=jnp.float32,
        )
        stats = pack_stats(top, total, lane)
        for j in range(GROUP):
            rows_ref[:, GROUP * r + j] = mixed[:, LANES * j : LANES * (j + 1)]
            rows_ref[:, GROUP * (REQ + r) + j] = stats
    packed_ref[...] = rows_ref[...].astype(jnp.bfloat16)


def merge_kernel(moved_ref, decode_ref):
    half = REQ * GROUP
    moved = moved_ref[...]
    stats = spread_stats(moved.reshape(-1, LANES))
    stats = stats.reshape(moved.shape[0], 2 * half, 2 * LANES)[:, half:]
    tops = stats[:, :, :LANES]
    scales = jnp.exp(tops - jnp.max(tops, axis=0, keepdims=True))
    mixed = jnp.sum(moved.astype(jnp.float32)[:, :half] * scales, axis=0)
    merged = (mixed / jnp.sum(stats[:, :, LANES:] * scales, axis=0)).astype(jnp.bfloat16)
    for r in range(REQ):
        for j in range(GROUP):
            row = GROUP * r + j
            decode_ref[r : r + 1, LANES * j : LANES * (j + 1)] = merged[row : row + 1]


def join_kernel(held_ref, received_ref, joined_ref):
    count = held_ref.shape[0]
    joined_ref[:count] = held_ref[...]
    joined_ref[count:] = received_ref[...]


def join_slots(held, received, params):
    vmem = pl.BlockSpec(memory_space=pltpu.VMEM)
    shape = (held.shape[0] + received.shape[0], *held.shape[1:])
    return pl.pallas_call(
        join_kernel,
        out_shape=jax.ShapeDtypeStruct(shape, held.dtype),
        in_specs=[vmem, vmem],
        out_specs=vmem,
        compiler_params=params,
        cost_estimate=pl.CostEstimate(flops=0, bytes_accessed=4 * held.size, transcendentals=0),
        name="join_slots",
    )(held, received)


def turn_kernel(turned_ref, query_ref):
    query_ref[...] = turned_ref[...].T


def placed_tokens(shape, rows):
    device = lax.axis_index("ctx")
    column = lax.broadcasted_iota(jnp.int32, shape, 1)
    place = lax.rem(column // rows, 4)
    low = jnp.zeros_like(column)
    for number in range(4):
        side = number // 2
        third = jnp.where((device & 1) ^ side == 1, 2, 4)
        base = (device & 7) ^ side
        low = jnp.where(place == number, base ^ third if number % 2 else base, low)
    return ((column // (rows * 4)) * 8 + low) * rows + lax.rem(column, rows)


def slot_tokens(shape, rows, slots, side):
    device = lax.axis_index("ctx")
    groups = slots // 2
    third = jnp.where((device & 1) ^ side == 1, 2, 4)
    column = lax.broadcasted_iota(jnp.int32, shape, 1)
    slot = column // rows
    odd = third == 2
    half = jnp.where(odd, slot & 1, slot // groups)
    high = jnp.where(odd, slot >> 1, slot & (groups - 1))
    owner = (device ^ side ^ (6 - third)) ^ (half * third)
    bits = groups.bit_length() - 1
    for step in range(bits):
        owner = owner ^ (((high >> step) & 1) * (8 << (bits - 1 - step)))
    return owner * rows + lax.rem(column, rows)


def tokens_kernel(n, rows, tokens_ref):
    shape = (1, tokens_ref.shape[1])
    tokens_ref[0:1] = placed_tokens(shape, rows)
    for side in range(2):
        tokens_ref[1 + side : 2 + side] = slot_tokens(shape, rows, n // 4, side)


def place_keys(refs, keys):
    device = lax.axis_index("ctx")
    slots, rows, _ = refs[0].shape
    groups = slots // 2
    bits = groups.bit_length() - 1

    def mask(high):
        return sum(8 << (bits - 1 - step) for step in range(bits) if (high >> step) & 1) // 8

    for side, ref in enumerate(refs):
        odd = (device & 1) ^ side == 1
        for t in range(slots):
            group = (device // 8) ^ jnp.where(odd, mask(t >> 1), mask(t & (groups - 1)))
            place = 2 * side + jnp.where(odd, t & 1, t // groups)
            keys[pl.ds(pl.multiple_of((group * 4 + place) * rows, rows), rows)] = ref[t]


def spread(column):
    return jnp.broadcast_to(column, (column.shape[0], LANES))


def block_weights(query, keys, token, first):
    scores = lax.dot_general(
        query, keys, (((1,), (1,)), ((), ())), preferred_element_type=jnp.float32
    )
    block, count = scores.shape
    row = first + lax.broadcasted_iota(jnp.int32, (block, count), 0)
    scores = jnp.where(token <= row, scores, NEG)
    top = jnp.max(scores, axis=1, keepdims=True)
    weights = jnp.exp2((scores - top) * (SCALE * LOG2E))
    total = jnp.sum(weights, axis=1, keepdims=True)
    mixed = jnp.dot(
        weights.astype(jnp.bfloat16), keys[:, :D_LAT], preferred_element_type=jnp.float32
    )
    return top, total, mixed


def early_kernel(tokens_ref, query_ref, own_ref, swap_ref, mixed_ref, keys):
    place_keys((own_ref, swap_ref), keys)
    lane = lax.broadcasted_iota(jnp.int32, (1, LANES), 1)
    block = 8 * own_ref.shape[1]
    count = query_ref.shape[0] // block
    columns = keys.shape[0] // count
    for index in range(count - 1, -1, -1):
        rows = slice(index * block, (index + 1) * block)
        upto = (index + 1) * columns
        top, total, mixed = block_weights(
            query_ref[rows], keys[:upto], tokens_ref[0:1, :upto], index * block
        )
        mixed_ref[rows, :D_LAT] = mixed.astype(jnp.bfloat16)
        mixed_ref[rows, D_LAT:] = pack_stats(top, total, lane).astype(jnp.bfloat16)


def fold_keys(query_ref, keys, token, stats_of, scores, weights):
    cut = scores.shape[0] * 3 // 4
    for part in (slice(cut, None), slice(0, cut)):
        scores[part] = lax.dot_general(
            query_ref[part], keys, (((1,), (1,)), ((), ())), preferred_element_type=jnp.float32
        )
    span, count = scores.shape
    block = min(SOFTMAX_ROWS, span)
    for first in range(0, span, block):
        rows = slice(first, first + block)
        row = first + lax.broadcasted_iota(jnp.int32, (block, count), 0)
        masked = jnp.where(token <= row, scores[rows], NEG)
        before, former = stats_of(rows)
        top = jnp.maximum(spread(jnp.max(masked, axis=1, keepdims=True)), before)
        total = jnp.zeros_like(top)
        for c in range(0, count, LANES):
            part = jnp.exp2((masked[:, c : c + LANES] - top) * (SCALE * LOG2E))
            weights[rows, c : c + LANES] = part.astype(jnp.bfloat16)
            total = total + part
        total = spread(jnp.sum(total, axis=1, keepdims=True))
        factor = jnp.exp2((before - top) * (SCALE * LOG2E))
        yield rows, top, factor, former * factor + total


def middle_kernel(
    tokens_ref,
    query_ref,
    own_ref,
    former_ref,
    mixed_ref,
    top_ref,
    total_ref,
    scores,
    weights,
    factors,
    stats,
):
    stats[...] = spread_stats(former_ref[:, D_LAT:])

    def stats_of(rows):
        return stats[rows, :LANES], stats[rows, LANES:]

    keys = own_ref[...].reshape(-1, own_ref.shape[2])
    token = tokens_ref[1:2, : keys.shape[0]]
    for rows, top, factor, total in fold_keys(query_ref, keys, token, stats_of, scores, weights):
        top_ref[rows] = top
        total_ref[rows] = total
        factors[rows] = factor
    values = keys[:, :D_LAT]
    block = 8 * own_ref.shape[1]
    for first in range(0, scores.shape[0], block):
        rows = slice(first, first + block)
        mixed = jnp.dot(weights[rows], values, preferred_element_type=jnp.float32)
        for c in range(0, D_LAT, LANES):
            part = slice(c, c + LANES)
            mixed_ref[rows, part] = (
                former_ref[rows, part].astype(jnp.float32) * factors[rows] + mixed[:, part]
            )


def late_kernel(
    tokens_ref,
    query_ref,
    swap_ref,
    former_ref,
    top_ref,
    total_ref,
    merged_ref,
    out_ref,
    decode_ref,
    scores,
    weights,
    factors,
    scales,
    blocks,
    sems,
):
    stores = [pltpu.make_async_copy(merged_ref, decode_ref, sems.at[0])]
    stores[0].start()

    def stats_of(rows):
        return top_ref[rows], total_ref[rows]

    keys = swap_ref[...].reshape(-1, swap_ref.shape[2])
    token = tokens_ref[2:3, : keys.shape[0]]
    for rows, _, factor, total in fold_keys(query_ref, keys, token, stats_of, scores, weights):
        scale = 1.0 / total
        scales[rows] = scale
        factors[rows] = factor * scale
    values = keys[:, :D_LAT]
    block = 8 * swap_ref.shape[1]
    for first in range(0, scores.shape[0], block):
        rows = slice(first, first + block)
        mixed = jnp.dot(weights[rows], values, preferred_element_type=jnp.float32)
        for c in range(0, D_LAT, LANES):
            part = slice(c, c + LANES)
            blocks[rows, part] = (
                former_ref[rows, part] * factors[rows] + mixed[:, part] * scales[rows]
            ).astype(jnp.bfloat16)
        span = pl.ds(first, block)
        store = pltpu.make_async_copy(blocks.at[span], out_ref.at[span], sems.at[len(stores)])
        store.start()
        stores.append(store)
    for store in stores:
        store.wait()


def shards(n, prefill_query, prefill_latent, decode_query, cache, lengths, page_table):
    span = prefill_query.shape[0]
    rows, width = prefill_latent.shape
    heads = decode_query.shape[1]
    vmem = pl.BlockSpec(memory_space=pltpu.VMEM)
    hbm = pl.BlockSpec(memory_space=pltpu.HBM)
    params = pltpu.CompilerParams(vmem_limit_bytes=VMEM_LIMIT)

    packed = pl.pallas_call(
        decode_kernel,
        out_shape=jax.ShapeDtypeStruct((heads, 2 * REQ * GROUP, LANES), jnp.bfloat16),
        in_specs=[hbm] * 5,
        out_specs=vmem,
        scratch_shapes=[
            pltpu.SMEM(page_table.shape[::-1], jnp.int32),
            pltpu.SMEM(lengths.shape, jnp.int32),
            pltpu.VMEM(decode_query.shape, jnp.bfloat16),
            pltpu.VMEM((REQ, width, cache.shape[1]), jnp.bfloat16),
            pltpu.VMEM((rows, width), jnp.bfloat16),
            pltpu.VMEM((heads, 2 * REQ * GROUP, LANES), jnp.float32),
            pltpu.SemaphoreType.DMA((4 + REQ,)),
        ],
        compiler_params=pltpu.CompilerParams(vmem_limit_bytes=VMEM_MOST),
        cost_estimate=pl.CostEstimate(
            flops=4 * cache.size * heads, bytes_accessed=2 * cache.size, transcendentals=0
        ),
        name="decode_part",
    )(page_table.T, lengths, decode_query, jnp.swapaxes(cache, 1, 2), prefill_latent)
    even_bits, odd_bits = bit_orders(n)
    held = prefill_latent[None]
    for step, (even, odd) in enumerate(zip(even_bits, odd_bits)):
        received = permute_bits(held, n, even, odd)
        if step < len(even_bits) - 1:
            held = join_slots(held, received, params)
    held_swap = permute_bits(held, n, 0, 0)
    received_swap = permute_bits(received, n, 0, 0)

    moved = lax.all_to_all(packed, "ctx", split_axis=0, concat_axis=0, tiled=True)

    query = pl.pallas_call(
        turn_kernel,
        out_shape=jax.ShapeDtypeStruct((span, width), jnp.bfloat16),
        in_specs=[vmem],
        out_specs=vmem,
        compiler_params=params,
        cost_estimate=pl.CostEstimate(flops=0, bytes_accessed=4 * span * width, transcendentals=0),
        name="turn_query",
    )(jnp.transpose(prefill_query, (1, 2, 0)).reshape(width, span))
    tokens = pl.pallas_call(
        functools.partial(tokens_kernel, n, rows),
        out_shape=jax.ShapeDtypeStruct((3, span // 2), jnp.int32),
        in_specs=[],
        out_specs=vmem,
        compiler_params=params,
        cost_estimate=pl.CostEstimate(flops=span, bytes_accessed=16, transcendentals=0),
        name="key_tokens",
    )()

    def cost(share):
        return pl.CostEstimate(
            flops=4 * span * span * width // share,
            bytes_accessed=4 * span * width,
            transcendentals=0,
        )

    sums = jax.ShapeDtypeStruct((span, D_LAT), jnp.float32)
    stat = jax.ShapeDtypeStruct((span, LANES), jnp.float32)
    quarter = span // 4
    scratch = [
        pltpu.VMEM((span, quarter), jnp.float32),
        pltpu.VMEM((span, quarter), jnp.bfloat16),
        pltpu.VMEM((span, LANES), jnp.float32),
    ]
    early = pl.pallas_call(
        early_kernel,
        out_shape=jax.ShapeDtypeStruct((span, D_LAT + LANES), jnp.bfloat16),
        in_specs=[vmem] * 4,
        out_specs=vmem,
        scratch_shapes=[pltpu.VMEM((span // 2, width), jnp.bfloat16)],
        compiler_params=params,
        cost_estimate=cost(2),
        name="prefill_early",
    )(tokens, query, held, held_swap)
    merged = pl.pallas_call(
        merge_kernel,
        out_shape=jax.ShapeDtypeStruct((REQ, D_LAT), jnp.bfloat16),
        in_specs=[vmem],
        out_specs=vmem,
        compiler_params=params,
        cost_estimate=pl.CostEstimate(flops=moved.size, bytes_accessed=16, transcendentals=0),
        name="decode_merge",
    )(moved)
    mixed, top, total = pl.pallas_call(
        middle_kernel,
        out_shape=(sums, stat, stat),
        in_specs=[vmem] * 4,
        out_specs=(vmem, vmem, vmem),
        scratch_shapes=scratch + [pltpu.VMEM((span, 2 * LANES), jnp.float32)],
        compiler_params=params,
        cost_estimate=cost(4),
        name="prefill_middle",
    )(tokens, query, received, early)
    prefill_out, decode_out = pl.pallas_call(
        late_kernel,
        out_shape=(
            jax.ShapeDtypeStruct((span, D_LAT), jnp.bfloat16),
            jax.ShapeDtypeStruct((REQ, D_LAT), jnp.bfloat16),
        ),
        in_specs=[vmem] * 7,
        out_specs=(hbm, hbm),
        scratch_shapes=scratch
        + [
            pltpu.VMEM((span, LANES), jnp.float32),
            pltpu.VMEM((span, D_LAT), jnp.bfloat16),
            pltpu.SemaphoreType.DMA((1 + n // 8,)),
        ],
        compiler_params=params,
        cost_estimate=cost(4),
        name="prefill_late",
    )(tokens, query, received_swap, mixed, top, total, merged)
    return prefill_out.reshape(span, 1, D_LAT), decode_out.reshape(REQ, 1, D_LAT)


def solution(mesh):
    n = mesh.shape["ctx"]
    in_specs = (
        P("groups", "ctx", None),
        P(("groups", "ctx"), None),
        P("groups", None, None),
        P("groups", "ctx", None),
        P("groups"),
        P("groups", None),
    )
    out_specs = (P("groups", "ctx", None), P("groups", "ctx", None))

    def body(*args):
        return shards(n, *args)

    return jax.shard_map(
        body, mesh=mesh, in_specs=in_specs, out_specs=out_specs, check_vma=False
    )
```

time: 50.2 us -> 45.6 us (0.908)
  other arithmetic: 3.16 us -> 0 us
  starting transfers between devices: 14.7 us -> 15.6 us
  local copies, waits for them, and re-layouts: 1.59 us -> 0.78 us
  Pallas kernels: 12.9 us -> 12.1 us
  waiting for transfers between devices: 16.8 us -> 16.1 us
    concatenate x3 -> x0, other arithmetic: 3.16 us -> none  [shards(): held = jnp.concatenate([held, received], axis=0)]
    ppermute x6, starting transfers between devices: 9.72 us -> 10.5 us  [permute_bits(): return lax.ppermute(rows, 'ctx', pairs)]
    unnamed x4, local copies, waits for them, and re-layouts: 1.59 us -> 0.78 us
    ppermute x6, waiting for transfers between devices: 9.21 us -> 8.7 us  [permute_bits(): return lax.ppermute(rows, 'ctx', pairs)]
    pallas_call x5 -> x9, Pallas kernels: 12.1 us -> 11.8 us  [the longest x1 3.26 us: shards(): pl.pallas_call(early_kernel, out_shape=jax.ShapeDtypeStruct((span, D_LAT...]
  transfers between devices with their start and end apart: 7 -> 7, of which waited for: 4 -> 4; matrix products, arithmetic and copies ran while one was open for 0% -> 0% of each run, Pallas kernels for 17% -> 22%
where the time goes in v2:
time: 45.6 us; the launch traced here: 45.3 us
  waiting for transfers between devices  16.1 us (35%)
  starting transfers between devices  15.6 us (34%)
  Pallas kernels  12.1 us (27%)
  local copies, waits for them, and re-layouts  0.78 us (2%)
  between operations  0.72 us (2%)
    ppermute x6, starting transfers between devices, permute_bits(): return lax.ppermute(rows, 'ctx', pairs)  10.5 us
    ppermute x6, waiting for transfers between devices, permute_bits(): return lax.ppermute(rows, 'ctx', pairs)  8.7 us
    all_to_all x1, waiting for transfers between devices, shards(): lax.all_to_all(packed, 'ctx', split_axis=0, concat_axis=0, tiled=True)  7.42 us
    all_to_all x1, starting transfers between devices, shards(): lax.all_to_all(packed, 'ctx', split_axis=0, concat_axis=0, tiled=True)  5.03 us
    pallas_call x1, Pallas kernels, shards(): pl.pallas_call(early_kernel, out_shape=jax.ShapeDtypeStruct((span, D_LAT...  3.26 us
    pallas_call x1, Pallas kernels, shards(): pl.pallas_call(decode_kernel, out_shape=jax.ShapeDtypeStruct((heads, 2 *...  3.21 us
    pallas_call x1, Pallas kernels, shards(): pl.pallas_call(middle_kernel, out_shape=(sums, stat, stat), in_specs=[vme...  2.59 us
    pallas_call x1, Pallas kernels, shards(): pl.pallas_call(late_kernel, out_shape=(jax.ShapeDtypeStruct((span, D_LAT)...  2.27 us
  transfers between devices with their start and end apart: 7, of which 4 were waited for; matrix products, arithmetic and copies ran while one was open for 0% of the time, Pallas kernels for 22%

profile of v2, /device:TPU:0, one launch (start us, length us, event | category | flops | bytes accessed | tf_op | source)
XLA Modules:
  0.0 45.3 jit_solution(15978893580060283537)
XLA Ops:
  0.6 4.1 %collective-permute-start = (bf16[1,32,576]{2,1,0:T(8,128)(2,1)}, bf16[1,32,576]{2,1,0:T(8,128)(2,1)S(1)}, u32[]{:S(2)}, u32[]{:S(2)}) collective-permute-start(bf16[1,32,576]{2,1,0:T(8,128)(2,1)} %bitcast.9), channel_id=1, source_target_pairs={{0,16},{1,3},{2,18},{3,1},{4,20},{5,7},{6,22},{7,5},{8,24},{9,11},... | collective-permute-start | bytes 110600 | tf_op jit(solution)/shard_map/ppermute | solution.py:33
  4.8 2.2 %collective-permute-done.received_ref = bf16[1,32,576]{2,1,0:T(8,128)(2,1)S(1)} collective-permute-done((bf16[1,32,576]{2,1,0:T(8,128)(2,1)}, bf16[1,32,576]{2,1,0:T(8,128)(2,1)S(1)}, u32[]{:S(2)}, u32[]{:S(2)}) %collective-permute-start) | collective-permute-done | bytes 36896 | tf_op jit(solution)/shard_map/ppermute | solution.py:33
  7.0 0.0 copy-start.1
  7.0 0.8 %copy-done.1 = bf16[32,576]{1,0:T(8,128)(2,1)S(1)} copy-done((bf16[32,576]{1,0:T(8,128)(2,1)S(1)}, bf16[32,576]{1,0:T(8,128)(2,1)}, u32[]{:S(2)}) %copy-start.1) | copy-done | bytes 36888
  7.7 0.0 copy-start
  7.8 2.0 %collective-permute-start.1 = (bf16[2,32,576]{2,1,0:T(8,128)(2,1)S(1)}, bf16[2,32,576]{2,1,0:T(8,128)(2,1)S(1)}, u32[]{:S(2)}, u32[]{:S(2)}) collective-permute-start(bf16[2,32,576]{2,1,0:T(8,128)(2,1)S(1)} %join_slots.3.held_ref), channel_id=1, source_target_pairs={{0,8},{1,17},{2,10},{3,19},{4,12},{5,21},{6,14},{7,23},{8,0},{9,25... | collective-permute-start | bytes 221192 | tf_op jit(solution)/shard_map/ppermute | solution.py:33
  9.7 2.5 %collective-permute-done.1.received_ref = bf16[2,32,576]{2,1,0:T(8,128)(2,1)S(1)} collective-permute-done((bf16[2,32,576]{2,1,0:T(8,128)(2,1)S(1)}, bf16[2,32,576]{2,1,0:T(8,128)(2,1)S(1)}, u32[]{:S(2)}, u32[]{:S(2)}) %collective-permute-start.1) | collective-permute-done | bytes 73760 | tf_op jit(solution)/shard_map/ppermute | solution.py:33
  12.3 1.9 %collective-permute-start.2 = (bf16[4,32,576]{2,1,0:T(8,128)(2,1)S(1)}, bf16[4,32,576]{2,1,0:T(8,128)(2,1)S(1)}, u32[]{:S(2)}, u32[]{:S(2)}) collective-permute-start(bf16[4,32,576]{2,1,0:T(8,128)(2,1)S(1)} %join_slots.4.held_ref), channel_id=1, source_target_pairs={{0,4},{1,9},{2,6},{3,11},{4,0},{5,13},{6,2},{7,15},{8,12},{9,1},{1... | collective-permute-start | bytes 442376 | tf_op jit(solution)/shard_map/ppermute | solution.py:33
  14.2 4.0 %collective-permute-done.2.received_ref = bf16[4,32,576]{2,1,0:T(8,128)(2,1)S(1)} collective-permute-done((bf16[4,32,576]{2,1,0:T(8,128)(2,1)S(1)}, bf16[4,32,576]{2,1,0:T(8,128)(2,1)S(1)}, u32[]{:S(2)}, u32[]{:S(2)}) %collective-permute-start.2) | collective-permute-done | bytes 147488 | tf_op jit(solution)/shard_map/ppermute | solution.py:33
  18.2 2.2 %collective-permute-start.3 = (bf16[8,32,576]{2,1,0:T(8,128)(2,1)S(1)}, bf16[8,32,576]{2,1,0:T(8,128)(2,1)}, u32[]{:S(2)}, u32[]{:S(2)}) collective-permute-start(bf16[8,32,576]{2,1,0:T(8,128)(2,1)S(1)} %join_slots.5.own_ref), channel_id=1, source_target_pairs={{0,2},{1,5},{2,0},{3,7},{4,6},{5,1},{6,4},{7,3},{8,10},{9,13},{10,... | collective-permute-start | bytes 884744 | tf_op jit(solution)/shard_map/ppermute | solution.py:33
  20.4 0.0 collective-permute-start.5
  20.4 3.2 %decode_part.1 = bf16[32,16,128]{2,1,0:T(8,128)(2,1)} custom-call(s32[2,64]{1,0:T(2,128)} %bitcast.12, s32[2]{0:T(128)} %lengths_hbm.1, bf16[2,32,576]{2,1,0:T(8,128)(2,1)} %query_hbm.1, bf16[2,576,512]{2,1,0:T(8,128)(2,1)} %bitcast.11, bf16[32,576]{1,0:T(8,128)(2,1)} %latent_hbm.1), custom_call_target="tpu_custom_call" | custom-call | flops 75497472 | bytes 1179648 | tf_op jit(solution)/shard_map/decode_part/pallas_call | solution.py:383
  23.6 5.0 %all-to-all-start = ((bf16[32,16,128]{2,1,0:T(8,128)(2,1)}), bf16[32,16,128]{2,1,0:T(8,128)(2,1)S(1)}, u32[]{:S(2)}, u32[]{:S(2)}) async-start(bf16[32,16,128]{2,1,0:T(8,128)(2,1)} %decode_part.1), calls=%async_computation | async-start | bytes 262144 | tf_op jit(solution)/shard_map/all_to_all | solution.py:412
  28.7 0.0 collective-permute-done.3.own_ref
  28.7 0.3 collective-permute-start.4
  29.0 0.0 copy-done
  29.0 0.4 turn_query.1.query_ref
  29.4 7.4 %all-to-all-done.moved_ref = bf16[32,16,128]{2,1,0:T(8,128)(2,1)S(1)} async-done(((bf16[32,16,128]{2,1,0:T(8,128)(2,1)}), bf16[32,16,128]{2,1,0:T(8,128)(2,1)S(1)}, u32[]{:S(2)}, u32[]{:S(2)}) %all-to-all-start) | async-done | bytes 131104 | tf_op jit(solution)/shard_map/all_to_all | solution.py:412
  36.9 0.3 decode_merge.1.merged_ref
  37.2 0.0 collective-permute-done.5.swap_ref
  37.2 3.3 %prefill_early.1.former_ref = bf16[1024,640]{1,0:T(8,128)(2,1)S(1)} custom-call(s32[3,512]{1,0:T(4,128)S(1)} %key_tokens.1.tokens_ref, bf16[1024,576]{1,0:T(8,128)(2,1)S(1)} %turn_query.1.query_ref, bf16[8,32,576]{2,1,0:T(8,128)(2,1)S(1)} %join_slots.5.own_ref, bf16[8,32,576]{2,1,0:T(8,128)(2,1)} %collective-permute-done.5.swap_ref), custom_call_target="tpu_custom_call" | custom-call | flops 1207959552 | bytes 2359296 | tf_op jit(solution)/shard_map/prefill_early/pallas_call | solution.py:448
  40.4 2.6 %prefill_middle.1 = (f32[1024,512]{1,0:T(8,128)S(1)}, f32[1024,128]{1,0:T(8,128)S(1)}, f32[1024,128]{1,0:T(8,128)S(1)}) custom-call(s32[3,512]{1,0:T(4,128)S(1)} %key_tokens.1.tokens_ref, bf16[1024,576]{1,0:T(8,128)(2,1)S(1)} %turn_query.1.query_ref, bf16[8,32,576]{2,1,0:T(8,128)(2,1)} %collective-permute-done.3.own_ref, ...), custom_call_target="tpu_custom_call" | custom-call | flops 603979776 | bytes 2359296 | tf_op jit(solution)/shard_map/prefill_middle/pallas_call | solution.py:467
  43.0 0.0 collective-permute-done.4.swap_ref
  43.0 2.3 %prefill_late.1 = (bf16[1024,512]{1,0:T(8,128)(2,1)}, bf16[2,512]{1,0:T(2,128)(2,1)}) custom-call(s32[3,512]{1,0:T(4,128)S(1)} %key_tokens.1.tokens_ref, bf16[1024,576]{1,0:T(8,128)(2,1)S(1)} %turn_query.1.query_ref, bf16[8,32,576]{2,1,0:T(8,128)(2,1)S(1)} %collective-permute-done.4.swap_ref, f32[1024,512]{1,0:T(8,128)S(1)} %get-tuple-element.7.former_ref, ...), custom_call_target="tpu_custom_call" | custom-call | flops 603979776 | bytes 2359296 | tf_op jit(solution)/shard_map/prefill_late/pallas_call | solution.py:477
  (4 shorter events, 0.1 us)
Async XLA Ops:
  0.6 6.3 %collective-permute-start = (bf16[1,32,576]{2,1,0:T(8,128)(2,1)}, bf16[1,32,576]{2,1,0:T(8,128)(2,1)S(1)}, u32[]{:S(2)}, u32[]{:S(2)}) collective-permute-start(bf16[1,32,576]{2,1,0:T(8,128)(2,1)} %bitcast.9), channel_id=1, source_target_pairs={{0,16},{1,3},{2,18},{3,1},{4,20},{5,7},{6,22},{7,5},{8,24},{9,11},... | collective-permute-start | bytes 110600 | tf_op jit(solution)/shard_map/ppermute | solution.py:33
  7.0 0.8 %copy-start.1 = (bf16[32,576]{1,0:T(8,128)(2,1)S(1)}, bf16[32,576]{1,0:T(8,128)(2,1)}, u32[]{:S(2)}) copy-start(bf16[32,576]{1,0:T(8,128)(2,1)} %latent_hbm.1) | copy-start | bytes 110596
  7.7 21.3 %copy-start = (bf16[1024,1,576]{0,2,1:T(8,128)(2,1)S(1)}, bf16[1024,1,576]{0,2,1:T(8,128)(2,1)}, u32[]{:S(2)}) copy-start(bf16[1024,1,576]{0,2,1:T(8,128)(2,1)} %param.6) | copy-start | bytes 3538948
  7.8 4.5 %collective-permute-start.1 = (bf16[2,32,576]{2,1,0:T(8,128)(2,1)S(1)}, bf16[2,32,576]{2,1,0:T(8,128)(2,1)S(1)}, u32[]{:S(2)}, u32[]{:S(2)}) collective-permute-start(bf16[2,32,576]{2,1,0:T(8,128)(2,1)S(1)} %join_slots.3.held_ref), channel_id=1, source_target_pairs={{0,8},{1,17},{2,10},{3,19},{4,12},{5,21},{6,14},{7,23},{8,0},{9,25... | collective-permute-start | bytes 221192 | tf_op jit(solution)/shard_map/ppermute | solution.py:33
  12.3 5.9 %collective-permute-start.2 = (bf16[4,32,576]{2,1,0:T(8,128)(2,1)S(1)}, bf16[4,32,576]{2,1,0:T(8,128)(2,1)S(1)}, u32[]{:S(2)}, u32[]{:S(2)}) collective-permute-start(bf16[4,32,576]{2,1,0:T(8,128)(2,1)S(1)} %join_slots.4.held_ref), channel_id=1, source_target_pairs={{0,4},{1,9},{2,6},{3,11},{4,0},{5,13},{6,2},{7,15},{8,12},{9,1},{1... | collective-permute-start | bytes 442376 | tf_op jit(solution)/shard_map/ppermute | solution.py:33
  18.2 10.5 %collective-permute-start.3 = (bf16[8,32,576]{2,1,0:T(8,128)(2,1)S(1)}, bf16[8,32,576]{2,1,0:T(8,128)(2,1)}, u32[]{:S(2)}, u32[]{:S(2)}) collective-permute-start(bf16[8,32,576]{2,1,0:T(8,128)(2,1)S(1)} %join_slots.5.own_ref), channel_id=1, source_target_pairs={{0,2},{1,5},{2,0},{3,7},{4,6},{5,1},{6,4},{7,3},{8,10},{9,13},{10,... | collective-permute-start | bytes 884744 | tf_op jit(solution)/shard_map/ppermute | solution.py:33
  20.4 16.8 %collective-permute-start.5 = (bf16[8,32,576]{2,1,0:T(8,128)(2,1)S(1)}, bf16[8,32,576]{2,1,0:T(8,128)(2,1)}, u32[]{:S(2)}, u32[]{:S(2)}) collective-permute-start(bf16[8,32,576]{2,1,0:T(8,128)(2,1)S(1)} %join_slots.5.own_ref), channel_id=1, source_target_pairs={{0,1},{1,0},{2,3},{3,2},{4,5},{5,4},{6,7},{7,6},{8,9},{9,8},{10,11... | collective-permute-start | bytes 884744 | tf_op jit(solution)/shard_map/ppermute | solution.py:33
  23.6 13.2 %all-to-all-start = ((bf16[32,16,128]{2,1,0:T(8,128)(2,1)}), bf16[32,16,128]{2,1,0:T(8,128)(2,1)S(1)}, u32[]{:S(2)}, u32[]{:S(2)}) async-start(bf16[32,16,128]{2,1,0:T(8,128)(2,1)} %decode_part.1), calls=%async_computation | async-start | bytes 262144 | tf_op jit(solution)/shard_map/all_to_all | solution.py:412
  28.7 14.4 %collective-permute-start.4 = (bf16[8,32,576]{2,1,0:T(8,128)(2,1)}, bf16[8,32,576]{2,1,0:T(8,128)(2,1)S(1)}, u32[]{:S(2)}, u32[]{:S(2)}) collective-permute-start(bf16[8,32,576]{2,1,0:T(8,128)(2,1)} %collective-permute-done.3.own_ref), channel_id=1, source_target_pairs={{0,1},{1,0},{2,3},{3,2},{4,5},{5,4},{6,7},{7,6},{8,9},{9,8},{10,11... | collective-permute-start | bytes 884744 | tf_op jit(solution)/shard_map/ppermute | solution.py:33

commit v3 on v2

--- a/solution.py
+++ b/solution.py
@@ -19,18 +19,12 @@
 NEG = -1e30
 SOFTMAX_ROWS = 64
 
-VMEM_LIMIT = 8 << 20
+VMEM_LIMIT = 12 << 20
 VMEM_MOST = 60 << 20
 
 
-def bit_orders(n):
-    bits = list(range(n.bit_length() - 2, 0, -1))
-    return bits, bits[-1:] + bits[:-1]
-
-
-def permute_bits(rows, n, even_bit, odd_bit):
-    pairs = [(i, i ^ (1 << (odd_bit if i & 1 else even_bit))) for i in range(n)]
-    return lax.ppermute(rows, "ctx", pairs)
+def permute_mask(rows, n, mask):
+    return lax.ppermute(rows, "ctx", [(i, i ^ mask) for i in range(n)])
 
 
 def split_parts(value):
@@ -176,93 +170,28 @@
     query_ref[...] = turned_ref[...].T
 
 
-def placed_tokens(shape, rows):
+def tokens_kernel(n, rows, tokens_ref):
     device = lax.axis_index("ctx")
-    column = lax.broadcasted_iota(jnp.int32, shape, 1)
-    place = lax.rem(column // rows, 4)
-    low = jnp.zeros_like(column)
-    for number in range(4):
-        side = number // 2
-        third = jnp.where((device & 1) ^ side == 1, 2, 4)
-        base = (device & 7) ^ side
-        low = jnp.where(place == number, base ^ third if number % 2 else base, low)
-    return ((column // (rows * 4)) * 8 + low) * rows + lax.rem(column, rows)
-
-
-def slot_tokens(shape, rows, slots, side):
-    device = lax.axis_index("ctx")
-    groups = slots // 2
-    third = jnp.where((device & 1) ^ side == 1, 2, 4)
+    shape = (1, tokens_ref.shape[1])
+    groups = n // 8
     column = lax.broadcasted_iota(jnp.int32, shape, 1)
     slot = column // rows
-    odd = third == 2
-    half = jnp.where(odd, slot & 1, slot // groups)
-    high = jnp.where(odd, slot >> 1, slot & (groups - 1))
-    owner = (device ^ side ^ (6 - third)) ^ (half * third)
+    group = jnp.full_like(column, device // 8)
     bits = groups.bit_length() - 1
     for step in range(bits):
-        owner = owner ^ (((high >> step) & 1) * (8 << (bits - 1 - step)))
-    return owner * rows + lax.rem(column, rows)
-
-
-def tokens_kernel(n, rows, tokens_ref):
-    shape = (1, tokens_ref.shape[1])
-    tokens_ref[0:1] = placed_tokens(shape, rows)
-    for side in range(2):
-        tokens_ref[1 + side : 2 + side] = slot_tokens(shape, rows, n // 4, side)
-
-
-def place_keys(refs, keys):
-    device = lax.axis_index("ctx")
-    slots, rows, _ = refs[0].shape
-    groups = slots // 2
-    bits = groups.bit_length() - 1
-
-    def mask(high):
-        return sum(8 << (bits - 1 - step) for step in range(bits) if (high >> step) & 1) // 8
-
-    for side, ref in enumerate(refs):
-        odd = (device & 1) ^ side == 1
-        for t in range(slots):
-            group = (device // 8) ^ jnp.where(odd, mask(t >> 1), mask(t & (groups - 1)))
-            place = 2 * side + jnp.where(odd, t & 1, t // groups)
-            keys[pl.ds(pl.multiple_of((group * 4 + place) * rows, rows), rows)] = ref[t]
+        group = group ^ (((slot >> step) & 1) << (bits - 1 - step))
+    number = slot // groups
+    for kernel, low in enumerate((number, 2 * (number + 1), 2 * (number + 1) + 1)):
+        owner = group * 8 + ((device & 7) ^ low)
+        tokens_ref[kernel : kernel + 1] = owner * rows + lax.rem(column, rows)
 
 
 def spread(column):
     return jnp.broadcast_to(column, (column.shape[0], LANES))
 
 
-def block_weights(query, keys, token, first):
-    scores = lax.dot_general(
-        query, keys, (((1,), (1,)), ((), ())), preferred_element_type=jnp.float32
-    )
-    block, count = scores.shape
-    row = first + lax.broadcasted_iota(jnp.int32, (block, count), 0)
-    scores = jnp.where(token <= row, scores, NEG)
-    top = jnp.max(scores, axis=1, keepdims=True)
-    weights = jnp.exp2((scores - top) * (SCALE * LOG2E))
-    total = jnp.sum(weights, axis=1, keepdims=True)
-    mixed = jnp.dot(
-        weights.astype(jnp.bfloat16), keys[:, :D_LAT], preferred_element_type=jnp.float32
-    )
-    return top, total, mixed
-
-
-def early_kernel(tokens_ref, query_ref, own_ref, swap_ref, mixed_ref, keys):
-    place_keys((own_ref, swap_ref), keys)
-    lane = lax.broadcasted_iota(jnp.int32, (1, LANES), 1)
-    block = 8 * own_ref.shape[1]
-    count = query_ref.shape[0] // block
-    columns = keys.shape[0] // count
-    for index in range(count - 1, -1, -1):
-        rows = slice(index * block, (index + 1) * block)
-        upto = (index + 1) * columns
-        top, total, mixed = block_weights(
-            query_ref[rows], keys[:upto], tokens_ref[0:1, :upto], index * block
-        )
-        mixed_ref[rows, :D_LAT] = mixed.astype(jnp.bfloat16)
-        mixed_ref[rows, D_LAT:] = pack_stats(top, total, lane).astype(jnp.bfloat16)
+def joined_keys(refs):
+    return jnp.concatenate([ref[...].reshape(-1, ref.shape[2]) for ref in refs], axis=0)
 
 
 def fold_keys(query_ref, keys, token, stats_of, scores, weights):
@@ -278,63 +207,84 @@
         row = first + lax.broadcasted_iota(jnp.int32, (block, count), 0)
         masked = jnp.where(token <= row, scores[rows], NEG)
         before, former = stats_of(rows)
-        top = jnp.maximum(spread(jnp.max(masked, axis=1, keepdims=True)), before)
+        top = spread(jnp.max(masked, axis=1, keepdims=True))
+        if before is not None:
+            top = jnp.maximum(top, before)
         total = jnp.zeros_like(top)
         for c in range(0, count, LANES):
             part = jnp.exp2((masked[:, c : c + LANES] - top) * (SCALE * LOG2E))
             weights[rows, c : c + LANES] = part.astype(jnp.bfloat16)
             total = total + part
         total = spread(jnp.sum(total, axis=1, keepdims=True))
-        factor = jnp.exp2((before - top) * (SCALE * LOG2E))
-        yield rows, top, factor, former * factor + total
+        factor = None
+        if before is not None:
+            factor = jnp.exp2((before - top) * (SCALE * LOG2E))
+            total = former * factor + total
+        yield rows, top, factor, total
+
+
+def value_blocks(weights, keys):
+    block = weights.shape[0] // 4
+    for first in range(0, weights.shape[0], block):
+        rows = slice(first, first + block)
+        yield rows, jnp.dot(weights[rows], keys[:, :D_LAT], preferred_element_type=jnp.float32)
+
+
+def early_kernel(
+    tokens_ref, query_ref, own_ref, swap_ref, mixed_ref, top_ref, total_ref, scores, weights
+):
+    keys = joined_keys((own_ref, swap_ref))
+    token = tokens_ref[0:1, : keys.shape[0]]
+    for rows, top, _, total in fold_keys(
+        query_ref, keys, token, lambda rows: (None, None), scores, weights
+    ):
+        top_ref[rows] = top
+        total_ref[rows] = total
+    for rows, mixed in value_blocks(weights, keys):
+        mixed_ref[rows] = mixed
 
 
 def middle_kernel(
     tokens_ref,
     query_ref,
-    own_ref,
+    x_ref,
+    y_ref,
+    diagonal_ref,
     former_ref,
+    before_ref,
+    counted_ref,
     mixed_ref,
     top_ref,
     total_ref,
     scores,
     weights,
     factors,
-    stats,
 ):
-    stats[...] = spread_stats(former_ref[:, D_LAT:])
-
     def stats_of(rows):
-        return stats[rows, :LANES], stats[rows, LANES:]
-
-    keys = own_ref[...].reshape(-1, own_ref.shape[2])
+        return before_ref[rows], counted_ref[rows]
+
+    keys = joined_keys((x_ref, y_ref, diagonal_ref))
     token = tokens_ref[1:2, : keys.shape[0]]
     for rows, top, factor, total in fold_keys(query_ref, keys, token, stats_of, scores, weights):
         top_ref[rows] = top
         total_ref[rows] = total
         factors[rows] = factor
-    values = keys[:, :D_LAT]
-    block = 8 * own_ref.shape[1]
-    for first in range(0, scores.shape[0], block):
-        rows = slice(first, first + block)
-        mixed = jnp.dot(weights[rows], values, preferred_element_type=jnp.float32)
+    for rows, mixed in value_blocks(weights, keys):
         for c in range(0, D_LAT, LANES):
             part = slice(c, c + LANES)
-            mixed_ref[rows, part] = (
-                former_ref[rows, part].astype(jnp.float32) * factors[rows] + mixed[:, part]
-            )
+            mixed_ref[rows, part] = former_ref[rows, part] * factors[rows] + mixed[:, part]
 
 
 def late_kernel(
     tokens_ref,
     query_ref,
-    swap_ref,
+    x_ref,
+    y_ref,
+    diagonal_ref,
     former_ref,
-    top_ref,
-    total_ref,
-    merged_ref,
+    before_ref,
+    counted_ref,
     out_ref,
-    decode_ref,
     scores,
     weights,
     factors,
@@ -342,29 +292,23 @@
     blocks,
     sems,
 ):
-    stores = [pltpu.make_async_copy(merged_ref, decode_ref, sems.at[0])]
-    stores[0].start()
-
     def stats_of(rows):
-        return top_ref[rows], total_ref[rows]
-
-    keys = swap_ref[...].reshape(-1, swap_ref.shape[2])
+        return before_ref[rows], counted_ref[rows]
+
+    keys = joined_keys((x_ref, y_ref, diagonal_ref))
     token = tokens_ref[2:3, : keys.shape[0]]
     for rows, _, factor, total in fold_keys(query_ref, keys, token, stats_of, scores, weights):
         scale = 1.0 / total
         scales[rows] = scale
         factors[rows] = factor * scale
-    values = keys[:, :D_LAT]
-    block = 8 * swap_ref.shape[1]
-    for first in range(0, scores.shape[0], block):
-        rows = slice(first, first + block)
-        mixed = jnp.dot(weights[rows], values, preferred_element_type=jnp.float32)
+    stores = []
+    for rows, mixed in value_blocks(weights, keys):
         for c in range(0, D_LAT, LANES):
             part = slice(c, c + LANES)
             blocks[rows, part] = (
                 former_ref[rows, part] * factors[rows] + mixed[:, part] * scales[rows]
             ).astype(jnp.bfloat16)
-        span = pl.ds(first, block)
+        span = pl.ds(rows.start, rows.stop - rows.start)
         store = pltpu.make_async_copy(blocks.at[span], out_ref.at[span], sems.at[len(stores)])
         store.start()
         stores.append(store)
@@ -400,14 +344,19 @@
         ),
         name="decode_part",
     )(page_table.T, lengths, decode_query, jnp.swapaxes(cache, 1, 2), prefill_latent)
-    even_bits, odd_bits = bit_orders(n)
+    groups = n // 8
     held = prefill_latent[None]
-    for step, (even, odd) in enumerate(zip(even_bits, odd_bits)):
-        received = permute_bits(held, n, even, odd)
-        if step < len(even_bits) - 1:
-            held = join_slots(held, received, params)
-    held_swap = permute_bits(held, n, 0, 0)
-    received_swap = permute_bits(received, n, 0, 0)
+    mask = n // 2
+    while mask >= 8:
+        received = permute_mask(held, n, mask)
+        held = join_slots(held, received, params)
+        mask //= 2
+    held_swap = permute_mask(held, n, 1)
+    received, received_swap = [], []
+    for number in range(1, 4):
+        received.append(permute_mask(held, n, 2 * number))
+    for number in range(1, 4):
+        received_swap.append(permute_mask(received[number - 1], n, 1))
 
     moved = lax.all_to_all(packed, "ctx", split_axis=0, concat_axis=0, tiled=True)
 
@@ -422,7 +371,7 @@
     )(jnp.transpose(prefill_query, (1, 2, 0)).reshape(width, span))
     tokens = pl.pallas_call(
         functools.partial(tokens_kernel, n, rows),
-        out_shape=jax.ShapeDtypeStruct((3, span // 2), jnp.int32),
+        out_shape=jax.ShapeDtypeStruct((3, 3 * groups * rows), jnp.int32),
         in_specs=[],
         out_specs=vmem,
         compiler_params=params,
@@ -438,24 +387,56 @@
         )
 
     sums = jax.ShapeDtypeStruct((span, D_LAT), jnp.float32)
-    stat = jax.ShapeDtypeStruct((span, LANES), jnp.float32)
-    quarter = span // 4
-    scratch = [
-        pltpu.VMEM((span, quarter), jnp.float32),
-        pltpu.VMEM((span, quarter), jnp.bfloat16),
-        pltpu.VMEM((span, LANES), jnp.float32),
-    ]
+    sums = (
+        jax.ShapeDtypeStruct((span, D_LAT), jnp.float32),
+        jax.ShapeDtypeStruct((span, LANES), jnp.float32),
+        jax.ShapeDtypeStruct((span, LANES), jnp.float32),
+    )
+
+    def scratch(count):
+        return [
+            pltpu.VMEM((span, count * groups * rows), jnp.float32),
+            pltpu.VMEM((span, count * groups * rows), jnp.bfloat16),
+        ]
+
+    factors = pltpu.VMEM((span, LANES), jnp.float32)
     early = pl.pallas_call(
         early_kernel,
-        out_shape=jax.ShapeDtypeStruct((span, D_LAT + LANES), jnp.bfloat16),
+        out_shape=sums,
         in_specs=[vmem] * 4,
-        out_specs=vmem,
-        scratch_shapes=[pltpu.VMEM((span // 2, width), jnp.bfloat16)],
-        compiler_params=params,
-        cost_estimate=cost(2),
+        out_specs=(vmem,) * 3,
+        scratch_shapes=scratch(2),
+        compiler_params=params,
+        cost_estimate=cost(4),
         name="prefill_early",
     )(tokens, query, held, held_swap)
-    merged = pl.pallas_call(
+    middle = pl.pallas_call(
+        middle_kernel,
+        out_shape=sums,
+        in_specs=[vmem] * 8,
+        out_specs=(vmem,) * 3,
+        scratch_shapes=scratch(3) + [factors],
+        compiler_params=params,
+        cost_estimate=cost(2),
+        name="prefill_middle",
+    )(tokens, query, *received, *early)
+    prefill_out = pl.pallas_call(
+        late_kernel,
+        out_shape=jax.ShapeDtypeStruct((span, D_LAT), jnp.bfloat16),
+        in_specs=[vmem] * 8,
+        out_specs=hbm,
+        scratch_shapes=scratch(3)
+        + [
+            factors,
+            factors,
+            pltpu.VMEM((span, D_LAT), jnp.bfloat16),
+            pltpu.SemaphoreType.DMA((4,)),
+        ],
+        compiler_params=params,
+        cost_estimate=cost(2),
+        name="prefill_late",
+    )(tokens, query, *received_swap, *middle)
+    decode_out = pl.pallas_call(
         merge_kernel,
         out_shape=jax.ShapeDtypeStruct((REQ, D_LAT), jnp.bfloat16),
         in_specs=[vmem],
@@ -464,34 +445,6 @@
         cost_estimate=pl.CostEstimate(flops=moved.size, bytes_accessed=16, transcendentals=0),
         name="decode_merge",
     )(moved)
-    mixed, top, total = pl.pallas_call(
-        middle_kernel,
-        out_shape=(sums, stat, stat),
-        in_specs=[vmem] * 4,
-        out_specs=(vmem, vmem, vmem),
-        scratch_shapes=scratch + [pltpu.VMEM((span, 2 * LANES), jnp.float32)],
-        compiler_params=params,
-        cost_estimate=cost(4),
-        name="prefill_middle",
-    )(tokens, query, received, early)
-    prefill_out, decode_out = pl.pallas_call(
-        late_kernel,
-        out_shape=(
-            jax.ShapeDtypeStruct((span, D_LAT), jnp.bfloat16),
-            jax.ShapeDtypeStruct((REQ, D_LAT), jnp.bfloat16),
-        ),
-        in_specs=[vmem] * 7,
-        out_specs=(hbm, hbm),
-        scratch_shapes=scratch
-        + [
-            pltpu.VMEM((span, LANES), jnp.float32),
-            pltpu.VMEM((span, D_LAT), jnp.bfloat16),
-            pltpu.SemaphoreType.DMA((1 + n // 8,)),
-        ],
-        compiler_params=params,
-        cost_estimate=cost(4),
-        name="prefill_late",
-    )(tokens, query, received_swap, mixed, top, total, merged)
     return prefill_out.reshape(span, 1, D_LAT), decode_out.reshape(REQ, 1, D_LAT)
 
 

time: 45.6 us -> 35.6 us (0.78)
  waiting for transfers between devices: 16.1 us -> 10.2 us
  starting transfers between devices: 15.6 us -> 13.9 us
  Pallas kernels: 12.1 us -> 10.6 us
  local copies, waits for them, and re-layouts: 0.78 us -> 0.01 us
    all_to_all x1, waiting for transfers between devices: 7.42 us -> 0.01 us  [shards(): lax.all_to_all(packed, 'ctx', split_axis=0, concat_axis=0, tiled=True)]
    pallas_call x3, Pallas kernels: 8.12 us -> 6.07 us  [the longest x1 2.73 us: shards(): pl.pallas_call(late_kernel, out_shape=jax.ShapeDtypeStruct((span, D_LAT),...]
    ppermute x6 -> x9, waiting for transfers between devices: 8.7 us -> 10.2 us  [permute_mask(): return lax.ppermute(rows, 'ctx', [(i, i ^ mask) for i in range(n)])]
    all_to_all x1, starting transfers between devices: 5.03 us -> 3.83 us  [shards(): lax.all_to_all(packed, 'ctx', split_axis=0, concat_axis=0, tiled=True)]
    unnamed x4, local copies, waits for them, and re-layouts: 0.78 us -> 0.01 us
    pallas_call x1, Pallas kernels: 0.29 us -> 0.87 us  [shards(): pl.pallas_call(merge_kernel, out_shape=jax.ShapeDtypeStruct((REQ, D_LAT),...]
    ppermute x6 -> x9, starting transfers between devices: 10.5 us -> 10 us  [permute_mask(): return lax.ppermute(rows, 'ctx', [(i, i ^ mask) for i in range(n)])]
  transfers between devices with their start and end apart: 7 -> 10, of which waited for: 4 -> 3; matrix products, arithmetic and copies ran while one was open for 0% -> 0% of each run, Pallas kernels for 22% -> 22%
where the time goes in v3:
time: 35.6 us; the launch traced here: 35.4 us
  starting transfers between devices  13.9 us (39%)
  Pallas kernels  10.6 us (30%)
  waiting for transfers between devices  10.2 us (29%)
  between operations  0.76 us (2%)
    ppermute x9, waiting for transfers between devices, permute_mask(): return lax.ppermute(rows, 'ctx', [(i, i ^ mask) for i in range(n)])  10.2 us
    ppermute x9, starting transfers between devices, permute_mask(): return lax.ppermute(rows, 'ctx', [(i, i ^ mask) for i in range(n)])  10 us
    all_to_all x1, starting transfers between devices, shards(): lax.all_to_all(packed, 'ctx', split_axis=0, concat_axis=0, tiled=True)  3.83 us
    pallas_call x1, Pallas kernels, shards(): pl.pallas_call(decode_kernel, out_shape=jax.ShapeDtypeStruct((heads, 2 *...  3.21 us
    pallas_call x1, Pallas kernels, shards(): pl.pallas_call(late_kernel, out_shape=jax.ShapeDtypeStruct((span, D_LAT),...  2.73 us
    pallas_call x1, Pallas kernels, shards(): pl.pallas_call(middle_kernel, out_shape=sums, in_specs=[vmem] * 8, out_sp...  2.02 us
    pallas_call x1, Pallas kernels, shards(): pl.pallas_call(early_kernel, out_shape=sums, in_specs=[vmem] * 4, out_spe...  1.33 us
    pallas_call x1, Pallas kernels, shards(): pl.pallas_call(merge_kernel, out_shape=jax.ShapeDtypeStruct((REQ, D_LAT),...  0.87 us
  transfers between devices with their start and end apart: 10, of which 3 were waited for; matrix products, arithmetic and copies ran while one was open for 0% of the time, Pallas kernels for 22%

profile of v3, /device:TPU:0, one launch (start us, length us, event | category | flops | bytes accessed | tf_op | source)
XLA Modules:
  0.0 35.4 jit_solution(14536733062904622256)
XLA Ops:
  0.6 0.0 copy-start.1
  0.6 0.0 copy-start
  0.7 4.1 %collective-permute-start = (bf16[1,32,576]{2,1,0:T(8,128)(2,1)}, bf16[1,32,576]{2,1,0:T(8,128)(2,1)S(1)}, u32[]{:S(2)}, u32[]{:S(2)}) collective-permute-start(bf16[1,32,576]{2,1,0:T(8,128)(2,1)} %bitcast.9), channel_id=1, source_target_pairs={{0,16},{1,17},{2,18},{3,19},{4,20},{5,21},{6,22},{7,23},{8,24},{9,... | collective-permute-start | bytes 110600 | tf_op jit(solution)/shard_map/ppermute | solution.py:27
  4.8 3.2 %decode_part.1 = bf16[32,16,128]{2,1,0:T(8,128)(2,1)} custom-call(s32[2,64]{1,0:T(2,128)} %bitcast.14, s32[2]{0:T(128)} %lengths_hbm.1, bf16[2,32,576]{2,1,0:T(8,128)(2,1)} %query_hbm.1, bf16[2,576,512]{2,1,0:T(8,128)(2,1)} %bitcast.11, bf16[32,576]{1,0:T(8,128)(2,1)} %latent_hbm.1), custom_call_target="tpu_custom_call" | custom-call | flops 75497472 | bytes 1179648 | tf_op jit(solution)/shard_map/decode_part/pallas_call | solution.py:327
  8.0 3.8 %all-to-all-start = ((bf16[32,16,128]{2,1,0:T(8,128)(2,1)}), bf16[32,16,128]{2,1,0:T(8,128)(2,1)S(1)}, u32[]{:S(2)}, u32[]{:S(2)}) async-start(bf16[32,16,128]{2,1,0:T(8,128)(2,1)} %decode_part.1), calls=%async_computation | async-start | bytes 262144 | tf_op jit(solution)/shard_map/all_to_all | solution.py:361
  11.8 0.0 collective-permute-done.received_ref
  11.9 0.0 copy-done.1
  11.9 1.8 %collective-permute-start.1 = (bf16[2,32,576]{2,1,0:T(8,128)(2,1)S(1)}, bf16[2,32,576]{2,1,0:T(8,128)(2,1)S(1)}, u32[]{:S(2)}, u32[]{:S(2)}) collective-permute-start(bf16[2,32,576]{2,1,0:T(8,128)(2,1)S(1)} %join_slots.2.held_ref), channel_id=1, source_target_pairs={{0,8},{1,9},{2,10},{3,11},{4,12},{5,13},{6,14},{7,15},{8,0},{9,1},... | collective-permute-start | bytes 221192 | tf_op jit(solution)/shard_map/ppermute | solution.py:27
  13.7 4.7 %collective-permute-done.1.received_ref = bf16[2,32,576]{2,1,0:T(8,128)(2,1)S(1)} collective-permute-done((bf16[2,32,576]{2,1,0:T(8,128)(2,1)S(1)}, bf16[2,32,576]{2,1,0:T(8,128)(2,1)S(1)}, u32[]{:S(2)}, u32[]{:S(2)}) %collective-permute-start.1) | collective-permute-done | bytes 73760 | tf_op jit(solution)/shard_map/ppermute | solution.py:27
  18.4 1.5 %collective-permute-start.2 = (bf16[4,32,576]{2,1,0:T(8,128)(2,1)S(1)}, bf16[4,32,576]{2,1,0:T(8,128)(2,1)S(1)}, u32[]{:S(2)}, u32[]{:S(2)}) collective-permute-start(bf16[4,32,576]{2,1,0:T(8,128)(2,1)S(1)} %join_slots.3.own_ref), channel_id=1, source_target_pairs={{0,2},{1,3},{2,0},{3,1},{4,6},{5,7},{6,4},{7,5},{8,10},{9,11},{10,... | collective-permute-start | bytes 442376 | tf_op jit(solution)/shard_map/ppermute | solution.py:27
  20.0 1.5 %collective-permute-start.4 = (bf16[4,32,576]{2,1,0:T(8,128)(2,1)S(1)}, bf16[4,32,576]{2,1,0:T(8,128)(2,1)S(1)}, u32[]{:S(2)}, u32[]{:S(2)}) collective-permute-start(bf16[4,32,576]{2,1,0:T(8,128)(2,1)S(1)} %join_slots.3.own_ref), channel_id=1, source_target_pairs={{0,4},{1,5},{2,6},{3,7},{4,0},{5,1},{6,2},{7,3},{8,12},{9,13},{10,... | collective-permute-start | bytes 442376 | tf_op jit(solution)/shard_map/ppermute | solution.py:27
  21.4 0.6 %collective-permute-start.6 = (bf16[4,32,576]{2,1,0:T(8,128)(2,1)S(1)}, bf16[4,32,576]{2,1,0:T(8,128)(2,1)S(1)}, u32[]{:S(2)}, u32[]{:S(2)}) collective-permute-start(bf16[4,32,576]{2,1,0:T(8,128)(2,1)S(1)} %join_slots.3.own_ref), channel_id=1, source_target_pairs={{0,6},{1,7},{2,4},{3,5},{4,2},{5,3},{6,0},{7,1},{8,14},{9,15},{10,... | collective-permute-start | bytes 442376 | tf_op jit(solution)/shard_map/ppermute | solution.py:27
  22.0 0.0 collective-permute-start.8
  22.0 0.0 copy-done
  22.0 0.4 %turn_query.1.query_ref = bf16[1024,576]{1,0:T(8,128)(2,1)S(1)} custom-call(bf16[576,1024]{1,0:T(8,128)(2,1)S(1)} %bitcast.8), custom_call_target="tpu_custom_call" | custom-call | bytes 2359296 | tf_op jit(solution)/shard_map/turn_query/pallas_call | solution.py:363
  22.4 0.0 all-to-all-done.moved_ref
  22.4 0.9 %decode_merge.1 = bf16[2,512]{1,0:T(2,128)(2,1)} custom-call(bf16[32,16,128]{2,1,0:T(8,128)(2,1)S(1)} %all-to-all-done.moved_ref), custom_call_target="tpu_custom_call" | custom-call | flops 65536 | bytes 16 | tf_op jit(solution)/shard_map/decode_merge/pallas_call | solution.py:439
  23.3 1.7 %collective-permute-done.2.x_ref = bf16[4,32,576]{2,1,0:T(8,128)(2,1)S(1)} collective-permute-done((bf16[4,32,576]{2,1,0:T(8,128)(2,1)S(1)}, bf16[4,32,576]{2,1,0:T(8,128)(2,1)S(1)}, u32[]{:S(2)}, u32[]{:S(2)}) %collective-permute-start.2) | collective-permute-done | bytes 147488 | tf_op jit(solution)/shard_map/ppermute | solution.py:27
  25.0 0.0 collective-permute-start.3
  25.0 3.8 %collective-permute-done.4.y_ref = bf16[4,32,576]{2,1,0:T(8,128)(2,1)S(1)} collective-permute-done((bf16[4,32,576]{2,1,0:T(8,128)(2,1)S(1)}, bf16[4,32,576]{2,1,0:T(8,128)(2,1)S(1)}, u32[]{:S(2)}, u32[]{:S(2)}) %collective-permute-start.4) | collective-permute-done | bytes 147488 | tf_op jit(solution)/shard_map/ppermute | solution.py:27
  28.8 0.0 collective-permute-start.5
  28.8 0.0 collective-permute-done.6.diagonal_ref
  28.8 0.5 %collective-permute-start.7 = (bf16[4,32,576]{2,1,0:T(8,128)(2,1)S(1)}, bf16[4,32,576]{2,1,0:T(8,128)(2,1)S(1)}, u32[]{:S(2)}, u32[]{:S(2)}) collective-permute-start(bf16[4,32,576]{2,1,0:T(8,128)(2,1)S(1)} %collective-permute-done.6.diagonal_ref), channel_id=1, source_target_pairs={{0,1},{1,0},{2,3},{3,2},{4,5},{5,4},{6,7},{7,6},{8,9},{9,8},{10,11... | collective-permute-start | bytes 442376 | tf_op jit(solution)/shard_map/ppermute | solution.py:27
  29.3 0.0 collective-permute-done.8.swap_ref
  29.3 1.3 %prefill_early.1 = (f32[1024,512]{1,0:T(8,128)S(1)}, f32[1024,128]{1,0:T(8,128)S(1)}, f32[1024,128]{1,0:T(8,128)S(1)}) custom-call(s32[3,384]{1,0:T(4,128)S(1)} %key_tokens.1.tokens_ref, bf16[1024,576]{1,0:T(8,128)(2,1)S(1)} %turn_query.1.query_ref, bf16[4,32,576]{2,1,0:T(8,128)(2,1)S(1)} %join_slots.3.own_ref, ...), custom_call_target="tpu_custom_call" | custom-call | flops 603979776 | bytes 2359296 | tf_op jit(solution)/shard_map/prefill_early/pallas_call | solution.py:403
  30.6 2.0 %prefill_middle.1 = (f32[1024,512]{1,0:T(8,128)S(1)}, f32[1024,128]{1,0:T(8,128)S(1)}, f32[1024,128]{1,0:T(8,128)S(1)}) custom-call(s32[3,384]{1,0:T(4,128)S(1)} %key_tokens.1.tokens_ref, bf16[1024,576]{1,0:T(8,128)(2,1)S(1)} %turn_query.1.query_ref, bf16[4,32,576]{2,1,0:T(8,128)(2,1)S(1)} %collective-permute-done.2.x_ref, ...), custom_call_target="tpu_custom_call" | custom-call | flops 1207959552 | bytes 2359296 | tf_op jit(solution)/shard_map/prefill_middle/pallas_call | solution.py:413
  32.6 0.0 collective-permute-done.3.x_ref
  32.7 0.0 collective-permute-done.5.y_ref
  32.7 0.0 collective-permute-done.7.diagonal_ref
  32.7 2.7 %prefill_late.1 = bf16[1024,512]{1,0:T(8,128)(2,1)} custom-call(s32[3,384]{1,0:T(4,128)S(1)} %key_tokens.1.tokens_ref, bf16[1024,576]{1,0:T(8,128)(2,1)S(1)} %turn_query.1.query_ref, bf16[4,32,576]{2,1,0:T(8,128)(2,1)S(1)} %collective-permute-done.3.x_ref, bf16[4,32,576]{2,1,0:T(8,128)(2,1)S(1)} %collective-permute-done.5.y_ref, ...), custom_call_target="tpu_custom_call" | custom-call | flops 1207959552 | bytes 2359296 | tf_op jit(solution)/shard_map/prefill_late/pallas_call | solution.py:423
  (3 shorter events, 0.1 us)
Async XLA Ops:
  0.6 11.2 %copy-start.1 = (bf16[32,576]{1,0:T(8,128)(2,1)S(1)}, bf16[32,576]{1,0:T(8,128)(2,1)}, u32[]{:S(2)}) copy-start(bf16[32,576]{1,0:T(8,128)(2,1)} %latent_hbm.1) | copy-start | bytes 110596
  0.6 21.4 %copy-start = (bf16[1024,1,576]{0,2,1:T(8,128)(2,1)S(1)}, bf16[1024,1,576]{0,2,1:T(8,128)(2,1)}, u32[]{:S(2)}) copy-start(bf16[1024,1,576]{0,2,1:T(8,128)(2,1)} %param.6) | copy-start | bytes 3538948
  0.7 11.2 %collective-permute-start = (bf16[1,32,576]{2,1,0:T(8,128)(2,1)}, bf16[1,32,576]{2,1,0:T(8,128)(2,1)S(1)}, u32[]{:S(2)}, u32[]{:S(2)}) collective-permute-start(bf16[1,32,576]{2,1,0:T(8,128)(2,1)} %bitcast.9), channel_id=1, source_target_pairs={{0,16},{1,17},{2,18},{3,19},{4,20},{5,21},{6,22},{7,23},{8,24},{9,... | collective-permute-start | bytes 110600 | tf_op jit(solution)/shard_map/ppermute | solution.py:27
  8.0 14.4 %all-to-all-start = ((bf16[32,16,128]{2,1,0:T(8,128)(2,1)}), bf16[32,16,128]{2,1,0:T(8,128)(2,1)S(1)}, u32[]{:S(2)}, u32[]{:S(2)}) async-start(bf16[32,16,128]{2,1,0:T(8,128)(2,1)} %decode_part.1), calls=%async_computation | async-start | bytes 262144 | tf_op jit(solution)/shard_map/all_to_all | solution.py:361
  11.9 6.5 %collective-permute-start.1 = (bf16[2,32,576]{2,1,0:T(8,128)(2,1)S(1)}, bf16[2,32,576]{2,1,0:T(8,128)(2,1)S(1)}, u32[]{:S(2)}, u32[]{:S(2)}) collective-permute-start(bf16[2,32,576]{2,1,0:T(8,128)(2,1)S(1)} %join_slots.2.held_ref), channel_id=1, source_target_pairs={{0,8},{1,9},{2,10},{3,11},{4,12},{5,13},{6,14},{7,15},{8,0},{9,1},... | collective-permute-start | bytes 221192 | tf_op jit(solution)/shard_map/ppermute | solution.py:27
  18.4 6.6 %collective-permute-start.2 = (bf16[4,32,576]{2,1,0:T(8,128)(2,1)S(1)}, bf16[4,32,576]{2,1,0:T(8,128)(2,1)S(1)}, u32[]{:S(2)}, u32[]{:S(2)}) collective-permute-start(bf16[4,32,576]{2,1,0:T(8,128)(2,1)S(1)} %join_slots.3.own_ref), channel_id=1, source_target_pairs={{0,2},{1,3},{2,0},{3,1},{4,6},{5,7},{6,4},{7,5},{8,10},{9,11},{10,... | collective-permute-start | bytes 442376 | tf_op jit(solution)/shard_map/ppermute | solution.py:27
  20.0 8.8 %collective-permute-start.4 = (bf16[4,32,576]{2,1,0:T(8,128)(2,1)S(1)}, bf16[4,32,576]{2,1,0:T(8,128)(2,1)S(1)}, u32[]{:S(2)}, u32[]{:S(2)}) collective-permute-start(bf16[4,32,576]{2,1,0:T(8,128)(2,1)S(1)} %join_slots.3.own_ref), channel_id=1, source_target_pairs={{0,4},{1,5},{2,6},{3,7},{4,0},{5,1},{6,2},{7,3},{8,12},{9,13},{10,... | collective-permute-start | bytes 442376 | tf_op jit(solution)/shard_map/ppermute | solution.py:27
  21.4 7.4 %collective-permute-start.6 = (bf16[4,32,576]{2,1,0:T(8,128)(2,1)S(1)}, bf16[4,32,576]{2,1,0:T(8,128)(2,1)S(1)}, u32[]{:S(2)}, u32[]{:S(2)}) collective-permute-start(bf16[4,32,576]{2,1,0:T(8,128)(2,1)S(1)} %join_slots.3.own_ref), channel_id=1, source_target_pairs={{0,6},{1,7},{2,4},{3,5},{4,2},{5,3},{6,0},{7,1},{8,14},{9,15},{10,... | collective-permute-start | bytes 442376 | tf_op jit(solution)/shard_map/ppermute | solution.py:27
  22.0 7.3 %collective-permute-start.8 = (bf16[4,32,576]{2,1,0:T(8,128)(2,1)S(1)}, bf16[4,32,576]{2,1,0:T(8,128)(2,1)S(1)}, u32[]{:S(2)}, u32[]{:S(2)}) collective-permute-start(bf16[4,32,576]{2,1,0:T(8,128)(2,1)S(1)} %join_slots.3.own_ref), channel_id=1, source_target_pairs={{0,1},{1,0},{2,3},{3,2},{4,5},{5,4},{6,7},{7,6},{8,9},{9,8},{10,11... | collective-permute-start | bytes 442376 | tf_op jit(solution)/shard_map/ppermute | solution.py:27
  25.0 7.6 %collective-permute-start.3 = (bf16[4,32,576]{2,1,0:T(8,128)(2,1)S(1)}, bf16[4,32,576]{2,1,0:T(8,128)(2,1)S(1)}, u32[]{:S(2)}, u32[]{:S(2)}) collective-permute-start(bf16[4,32,576]{2,1,0:T(8,128)(2,1)S(1)} %collective-permute-done.2.x_ref), channel_id=1, source_target_pairs={{0,1},{1,0},{2,3},{3,2},{4,5},{5,4},{6,7},{7,6},{8,9},{9,8},{10,11... | collective-permute-start | bytes 442376 | tf_op jit(solution)/shard_map/ppermute | solution.py:27
  28.8 3.9 %collective-permute-start.5 = (bf16[4,32,576]{2,1,0:T(8,128)(2,1)S(1)}, bf16[4,32,576]{2,1,0:T(8,128)(2,1)S(1)}, u32[]{:S(2)}, u32[]{:S(2)}) collective-permute-start(bf16[4,32,576]{2,1,0:T(8,128)(2,1)S(1)} %collective-permute-done.4.y_ref), channel_id=1, source_target_pairs={{0,1},{1,0},{2,3},{3,2},{4,5},{5,4},{6,7},{7,6},{8,9},{9,8},{10,11... | collective-permute-start | bytes 442376 | tf_op jit(solution)/shard_map/ppermute | solution.py:27
  28.8 3.9 %collective-permute-start.7 = (bf16[4,32,576]{2,1,0:T(8,128)(2,1)S(1)}, bf16[4,32,576]{2,1,0:T(8,128)(2,1)S(1)}, u32[]{:S(2)}, u32[]{:S(2)}) collective-permute-start(bf16[4,32,576]{2,1,0:T(8,128)(2,1)S(1)} %collective-permute-done.6.diagonal_ref), channel_id=1, source_target_pairs={{0,1},{1,0},{2,3},{3,2},{4,5},{5,4},{6,7},{7,6},{8,9},{9,8},{10,11... | collective-permute-start | bytes 442376 | tf_op jit(solution)/shard_map/ppermute | solution.py:27

commit v4 on v3

--- a/solution.py
+++ b/solution.py
@@ -12,12 +12,11 @@
 POOL = 16
 REQ = 2
 LANES = 128
-GROUP = D_LAT // LANES
 
 SCALE = 192.0 ** (-0.5)
 LOG2E = 1.4426950408889634
 NEG = -1e30
-SOFTMAX_ROWS = 64
+SOFTMAX_ROWS = 32
 
 VMEM_LIMIT = 12 << 20
 VMEM_MOST = 60 << 20
@@ -125,25 +124,21 @@
             preferred_element_type=jnp.float32,
         )
         stats = pack_stats(top, total, lane)
-        for j in range(GROUP):
-            rows_ref[:, GROUP * r + j] = mixed[:, LANES * j : LANES * (j + 1)]
-            rows_ref[:, GROUP * (REQ + r) + j] = stats
+        rows_ref[:, r, :D_LAT] = mixed
+        rows_ref[:, r, D_LAT:] = stats
     packed_ref[...] = rows_ref[...].astype(jnp.bfloat16)
 
 
 def merge_kernel(moved_ref, decode_ref):
-    half = REQ * GROUP
-    moved = moved_ref[...]
-    stats = spread_stats(moved.reshape(-1, LANES))
-    stats = stats.reshape(moved.shape[0], 2 * half, 2 * LANES)[:, half:]
+    senders = moved_ref.shape[0]
+    stats = spread_stats(moved_ref[:, :, D_LAT:].reshape(-1, LANES))
+    stats = stats.reshape(senders, REQ, 2 * LANES)
     tops = stats[:, :, :LANES]
     scales = jnp.exp(tops - jnp.max(tops, axis=0, keepdims=True))
-    mixed = jnp.sum(moved.astype(jnp.float32)[:, :half] * scales, axis=0)
-    merged = (mixed / jnp.sum(stats[:, :, LANES:] * scales, axis=0)).astype(jnp.bfloat16)
-    for r in range(REQ):
-        for j in range(GROUP):
-            row = GROUP * r + j
-            decode_ref[r : r + 1, LANES * j : LANES * (j + 1)] = merged[row : row + 1]
+    total = jnp.sum(stats[:, :, LANES:] * scales, axis=0)
+    for c in range(0, D_LAT, LANES):
+        mixed = jnp.sum(moved_ref[:, :, c : c + LANES].astype(jnp.float32) * scales, axis=0)
+        decode_ref[:, c : c + LANES] = (mixed / total).astype(jnp.bfloat16)
 
 
 def join_kernel(held_ref, received_ref, joined_ref):
@@ -195,7 +190,7 @@
 
 
 def fold_keys(query_ref, keys, token, stats_of, scores, weights):
-    cut = scores.shape[0] * 3 // 4
+    cut = scores.shape[0] // 2
     for part in (slice(cut, None), slice(0, cut)):
         scores[part] = lax.dot_general(
             query_ref[part], keys, (((1,), (1,)), ((), ())), preferred_element_type=jnp.float32
@@ -326,7 +321,7 @@
 
     packed = pl.pallas_call(
         decode_kernel,
-        out_shape=jax.ShapeDtypeStruct((heads, 2 * REQ * GROUP, LANES), jnp.bfloat16),
+        out_shape=jax.ShapeDtypeStruct((heads, REQ, D_LAT + LANES), jnp.bfloat16),
         in_specs=[hbm] * 5,
         out_specs=vmem,
         scratch_shapes=[
@@ -335,7 +330,7 @@
             pltpu.VMEM(decode_query.shape, jnp.bfloat16),
             pltpu.VMEM((REQ, width, cache.shape[1]), jnp.bfloat16),
             pltpu.VMEM((rows, width), jnp.bfloat16),
-            pltpu.VMEM((heads, 2 * REQ * GROUP, LANES), jnp.float32),
+            pltpu.VMEM((heads, REQ, D_LAT + LANES), jnp.float32),
             pltpu.SemaphoreType.DMA((4 + REQ,)),
         ],
         compiler_params=pltpu.CompilerParams(vmem_limit_bytes=VMEM_MOST),

time: 35.6 us -> 36.8 us (1.034)
  starting transfers between devices: 13.9 us -> 14.9 us
  local copies, waits for them, and re-layouts: 0.01 us -> 0.78 us
  waiting for transfers between devices: 10.2 us -> 9.72 us
    ppermute x9, waiting for transfers between devices: 10.2 us -> 6.08 us  [permute_mask(): return lax.ppermute(rows, 'ctx', [(i, i ^ mask) for i in range(n)])]
    all_to_all x1, waiting for transfers between devices: 0.01 us -> 3.65 us  [shards(): lax.all_to_all(packed, 'ctx', split_axis=0, concat_axis=0, tiled=True)]
    all_to_all x1, starting transfers between devices: 3.83 us -> 5.17 us  [shards(): lax.all_to_all(packed, 'ctx', split_axis=0, concat_axis=0, tiled=True)]
    unnamed x4, local copies, waits for them, and re-layouts: 0.01 us -> 0.78 us
  transfers between devices with their start and end apart: 10 -> 10, of which waited for: 3 -> 3; matrix products, arithmetic and copies ran while one was open for 0% -> 0% of each run, Pallas kernels for 22% -> 21%
where the time goes in v4:
time: 36.8 us; the launch traced here: 36.6 us
  starting transfers between devices  14.9 us (40%)
  Pallas kernels  10.4 us (28%)
  waiting for transfers between devices  9.72 us (26%)
  local copies, waits for them, and re-layouts  0.78 us (2%)
  between operations  0.73 us (2%)
    ppermute x9, starting transfers between devices, permute_mask(): return lax.ppermute(rows, 'ctx', [(i, i ^ mask) for i in range(n)])  9.74 us
    ppermute x9, waiting for transfers between devices, permute_mask(): return lax.ppermute(rows, 'ctx', [(i, i ^ mask) for i in range(n)])  6.08 us
    all_to_all x1, starting transfers between devices, shards(): lax.all_to_all(packed, 'ctx', split_axis=0, concat_axis=0, tiled=True)  5.17 us
    all_to_all x1, waiting for transfers between devices, shards(): lax.all_to_all(packed, 'ctx', split_axis=0, concat_axis=0, tiled=True)  3.65 us
    pallas_call x1, Pallas kernels, shards(): pl.pallas_call(decode_kernel, out_shape=jax.ShapeDtypeStruct((heads, REQ,...  3.17 us
    pallas_call x1, Pallas kernels, shards(): pl.pallas_call(late_kernel, out_shape=jax.ShapeDtypeStruct((span, D_LAT),...  2.84 us
    pallas_call x1, Pallas kernels, shards(): pl.pallas_call(middle_kernel, out_shape=sums, in_specs=[vmem] * 8, out_sp...  2.06 us
    pallas_call x1, Pallas kernels, shards(): pl.pallas_call(early_kernel, out_shape=sums, in_specs=[vmem] * 4, out_spe...  1.06 us
  transfers between devices with their start and end apart: 10, of which 3 were waited for; matrix products, arithmetic and copies ran while one was open for 0% of the time, Pallas kernels for 21%

profile of v4, /device:TPU:0, one launch (start us, length us, event | category | flops | bytes accessed | tf_op | source)
XLA Modules:
  0.0 36.6 jit_solution(10920840126763880148)
XLA Ops:
  0.6 0.0 copy-start
  0.6 4.1 %collective-permute-start = (bf16[1,32,576]{2,1,0:T(8,128)(2,1)}, bf16[1,32,576]{2,1,0:T(8,128)(2,1)S(1)}, u32[]{:S(2)}, u32[]{:S(2)}) collective-permute-start(bf16[1,32,576]{2,1,0:T(8,128)(2,1)} %bitcast.9), channel_id=1, source_target_pairs={{0,16},{1,17},{2,18},{3,19},{4,20},{5,21},{6,22},{7,23},{8,24},{9,... | collective-permute-start | bytes 110600 | tf_op jit(solution)/shard_map/ppermute | solution.py:26
  4.8 2.6 %collective-permute-done.received_ref = bf16[1,32,576]{2,1,0:T(8,128)(2,1)S(1)} collective-permute-done((bf16[1,32,576]{2,1,0:T(8,128)(2,1)}, bf16[1,32,576]{2,1,0:T(8,128)(2,1)S(1)}, u32[]{:S(2)}, u32[]{:S(2)}) %collective-permute-start) | collective-permute-done | bytes 36896 | tf_op jit(solution)/shard_map/ppermute | solution.py:26
  7.4 0.0 copy-start.1
  7.4 0.8 %copy-done.1 = bf16[32,576]{1,0:T(8,128)(2,1)S(1)} copy-done((bf16[32,576]{1,0:T(8,128)(2,1)S(1)}, bf16[32,576]{1,0:T(8,128)(2,1)}, u32[]{:S(2)}) %copy-start.1) | copy-done | bytes 36888
  8.2 1.5 %collective-permute-start.1 = (bf16[2,32,576]{2,1,0:T(8,128)(2,1)S(1)}, bf16[2,32,576]{2,1,0:T(8,128)(2,1)S(1)}, u32[]{:S(2)}, u32[]{:S(2)}) collective-permute-start(bf16[2,32,576]{2,1,0:T(8,128)(2,1)S(1)} %join_slots.2.held_ref), channel_id=1, source_target_pairs={{0,8},{1,9},{2,10},{3,11},{4,12},{5,13},{6,14},{7,15},{8,0},{9,1},... | collective-permute-start | bytes 221192 | tf_op jit(solution)/shard_map/ppermute | solution.py:26
  9.7 3.2 %decode_part.1 = bf16[32,2,640]{2,1,0:T(2,128)(2,1)} custom-call(s32[2,64]{1,0:T(2,128)} %bitcast.14, s32[2]{0:T(128)} %lengths_hbm.1, bf16[2,32,576]{2,1,0:T(8,128)(2,1)} %query_hbm.1, bf16[2,576,512]{2,1,0:T(8,128)(2,1)} %bitcast.11, bf16[32,576]{1,0:T(8,128)(2,1)} %latent_hbm.1), custom_call_target="tpu_custom_call" | custom-call | flops 75497472 | bytes 1179648 | tf_op jit(solution)/shard_map/decode_part/pallas_call | solution.py:322
  12.9 5.2 %all-to-all-start = ((bf16[32,2,640]{2,1,0:T(2,128)(2,1)}), bf16[32,2,640]{2,1,0:T(2,128)(2,1)S(1)}, u32[]{:S(2)}, u32[]{:S(2)}) async-start(bf16[32,2,640]{2,1,0:T(2,128)(2,1)} %decode_part.1), calls=%async_computation | async-start | bytes 163840 | tf_op jit(solution)/shard_map/all_to_all | solution.py:356
  18.1 0.0 collective-permute-done.1.received_ref
  18.1 1.8 %collective-permute-start.2 = (bf16[4,32,576]{2,1,0:T(8,128)(2,1)S(1)}, bf16[4,32,576]{2,1,0:T(8,128)(2,1)S(1)}, u32[]{:S(2)}, u32[]{:S(2)}) collective-permute-start(bf16[4,32,576]{2,1,0:T(8,128)(2,1)S(1)} %join_slots.3.own_ref), channel_id=1, source_target_pairs={{0,2},{1,3},{2,0},{3,1},{4,6},{5,7},{6,4},{7,5},{8,10},{9,11},{10,... | collective-permute-start | bytes 442376 | tf_op jit(solution)/shard_map/ppermute | solution.py:26
  19.9 1.5 %collective-permute-start.4 = (bf16[4,32,576]{2,1,0:T(8,128)(2,1)S(1)}, bf16[4,32,576]{2,1,0:T(8,128)(2,1)S(1)}, u32[]{:S(2)}, u32[]{:S(2)}) collective-permute-start(bf16[4,32,576]{2,1,0:T(8,128)(2,1)S(1)} %join_slots.3.own_ref), channel_id=1, source_target_pairs={{0,4},{1,5},{2,6},{3,7},{4,0},{5,1},{6,2},{7,3},{8,12},{9,13},{10,... | collective-permute-start | bytes 442376 | tf_op jit(solution)/shard_map/ppermute | solution.py:26
  21.4 0.3 collective-permute-start.6
  21.7 0.0 collective-permute-start.8
  21.7 0.0 copy-done
  21.7 0.4 %turn_query.1.query_ref = bf16[1024,576]{1,0:T(8,128)(2,1)S(1)} custom-call(bf16[576,1024]{1,0:T(8,128)(2,1)S(1)} %bitcast.8), custom_call_target="tpu_custom_call" | custom-call | bytes 2359296 | tf_op jit(solution)/shard_map/turn_query/pallas_call | solution.py:358
  22.1 3.6 %all-to-all-done.moved_ref = bf16[32,2,640]{2,1,0:T(2,128)(2,1)S(1)} async-done(((bf16[32,2,640]{2,1,0:T(2,128)(2,1)}), bf16[32,2,640]{2,1,0:T(2,128)(2,1)S(1)}, u32[]{:S(2)}, u32[]{:S(2)}) %all-to-all-start) | async-done | bytes 81952 | tf_op jit(solution)/shard_map/all_to_all | solution.py:356
  25.8 0.9 %decode_merge.1 = bf16[2,512]{1,0:T(2,128)(2,1)} custom-call(bf16[32,2,640]{2,1,0:T(2,128)(2,1)S(1)} %all-to-all-done.moved_ref), custom_call_target="tpu_custom_call" | custom-call | flops 40960 | bytes 16 | tf_op jit(solution)/shard_map/decode_merge/pallas_call | solution.py:434
  26.6 0.0 collective-permute-done.2.x_ref
  26.6 0.0 collective-permute-start.3
  26.6 3.4 %collective-permute-done.4.y_ref = bf16[4,32,576]{2,1,0:T(8,128)(2,1)S(1)} collective-permute-done((bf16[4,32,576]{2,1,0:T(8,128)(2,1)S(1)}, bf16[4,32,576]{2,1,0:T(8,128)(2,1)S(1)}, u32[]{:S(2)}, u32[]{:S(2)}) %collective-permute-start.4) | collective-permute-done | bytes 147488 | tf_op jit(solution)/shard_map/ppermute | solution.py:26
  30.1 0.0 collective-permute-start.5
  30.1 0.0 collective-permute-done.6.diagonal_ref
  30.1 0.5 %collective-permute-start.7 = (bf16[4,32,576]{2,1,0:T(8,128)(2,1)S(1)}, bf16[4,32,576]{2,1,0:T(8,128)(2,1)S(1)}, u32[]{:S(2)}, u32[]{:S(2)}) collective-permute-start(bf16[4,32,576]{2,1,0:T(8,128)(2,1)S(1)} %collective-permute-done.6.diagonal_ref), channel_id=1, source_target_pairs={{0,1},{1,0},{2,3},{3,2},{4,5},{5,4},{6,7},{7,6},{8,9},{9,8},{10,11... | collective-permute-start | bytes 442376 | tf_op jit(solution)/shard_map/ppermute | solution.py:26
  30.6 0.0 collective-permute-done.8.swap_ref
  30.6 1.1 %prefill_early.1 = (f32[1024,512]{1,0:T(8,128)S(1)}, f32[1024,128]{1,0:T(8,128)S(1)}, f32[1024,128]{1,0:T(8,128)S(1)}) custom-call(s32[3,384]{1,0:T(4,128)S(1)} %key_tokens.1.tokens_ref, bf16[1024,576]{1,0:T(8,128)(2,1)S(1)} %turn_query.1.query_ref, bf16[4,32,576]{2,1,0:T(8,128)(2,1)S(1)} %join_slots.3.own_ref, ...), custom_call_target="tpu_custom_call" | custom-call | flops 603979776 | bytes 2359296 | tf_op jit(solution)/shard_map/prefill_early/pallas_call | solution.py:398
  31.6 2.1 %prefill_middle.1 = (f32[1024,512]{1,0:T(8,128)S(1)}, f32[1024,128]{1,0:T(8,128)S(1)}, f32[1024,128]{1,0:T(8,128)S(1)}) custom-call(s32[3,384]{1,0:T(4,128)S(1)} %key_tokens.1.tokens_ref, bf16[1024,576]{1,0:T(8,128)(2,1)S(1)} %turn_query.1.query_ref, bf16[4,32,576]{2,1,0:T(8,128)(2,1)S(1)} %collective-permute-done.2.x_ref, ...), custom_call_target="tpu_custom_call" | custom-call | flops 1207959552 | bytes 2359296 | tf_op jit(solution)/shard_map/prefill_middle/pallas_call | solution.py:408
  33.7 0.0 collective-permute-done.3.x_ref
  33.7 0.0 collective-permute-done.5.y_ref
  33.7 0.0 collective-permute-done.7.diagonal_ref
  33.7 2.8 %prefill_late.1 = bf16[1024,512]{1,0:T(8,128)(2,1)} custom-call(s32[3,384]{1,0:T(4,128)S(1)} %key_tokens.1.tokens_ref, bf16[1024,576]{1,0:T(8,128)(2,1)S(1)} %turn_query.1.query_ref, bf16[4,32,576]{2,1,0:T(8,128)(2,1)S(1)} %collective-permute-done.3.x_ref, bf16[4,32,576]{2,1,0:T(8,128)(2,1)S(1)} %collective-permute-done.5.y_ref, ...), custom_call_target="tpu_custom_call" | custom-call | flops 1207959552 | bytes 2359296 | tf_op jit(solution)/shard_map/prefill_late/pallas_call | solution.py:418
  (3 shorter events, 0.1 us)
Async XLA Ops:
  0.6 21.1 %copy-start = (bf16[1024,1,576]{0,2,1:T(8,128)(2,1)S(1)}, bf16[1024,1,576]{0,2,1:T(8,128)(2,1)}, u32[]{:S(2)}) copy-start(bf16[1024,1,576]{0,2,1:T(8,128)(2,1)} %param.6) | copy-start | bytes 3538948
  0.6 6.8 %collective-permute-start = (bf16[1,32,576]{2,1,0:T(8,128)(2,1)}, bf16[1,32,576]{2,1,0:T(8,128)(2,1)S(1)}, u32[]{:S(2)}, u32[]{:S(2)}) collective-permute-start(bf16[1,32,576]{2,1,0:T(8,128)(2,1)} %bitcast.9), channel_id=1, source_target_pairs={{0,16},{1,17},{2,18},{3,19},{4,20},{5,21},{6,22},{7,23},{8,24},{9,... | collective-permute-start | bytes 110600 | tf_op jit(solution)/shard_map/ppermute | solution.py:26
  7.4 0.8 %copy-start.1 = (bf16[32,576]{1,0:T(8,128)(2,1)S(1)}, bf16[32,576]{1,0:T(8,128)(2,1)}, u32[]{:S(2)}) copy-start(bf16[32,576]{1,0:T(8,128)(2,1)} %latent_hbm.1) | copy-start | bytes 110596
  8.2 9.9 %collective-permute-start.1 = (bf16[2,32,576]{2,1,0:T(8,128)(2,1)S(1)}, bf16[2,32,576]{2,1,0:T(8,128)(2,1)S(1)}, u32[]{:S(2)}, u32[]{:S(2)}) collective-permute-start(bf16[2,32,576]{2,1,0:T(8,128)(2,1)S(1)} %join_slots.2.held_ref), channel_id=1, source_target_pairs={{0,8},{1,9},{2,10},{3,11},{4,12},{5,13},{6,14},{7,15},{8,0},{9,1},... | collective-permute-start | bytes 221192 | tf_op jit(solution)/shard_map/ppermute | solution.py:26
  12.9 12.9 %all-to-all-start = ((bf16[32,2,640]{2,1,0:T(2,128)(2,1)}), bf16[32,2,640]{2,1,0:T(2,128)(2,1)S(1)}, u32[]{:S(2)}, u32[]{:S(2)}) async-start(bf16[32,2,640]{2,1,0:T(2,128)(2,1)} %decode_part.1), calls=%async_computation | async-start | bytes 163840 | tf_op jit(solution)/shard_map/all_to_all | solution.py:356
  18.1 8.5 %collective-permute-start.2 = (bf16[4,32,576]{2,1,0:T(8,128)(2,1)S(1)}, bf16[4,32,576]{2,1,0:T(8,128)(2,1)S(1)}, u32[]{:S(2)}, u32[]{:S(2)}) collective-permute-start(bf16[4,32,576]{2,1,0:T(8,128)(2,1)S(1)} %join_slots.3.own_ref), channel_id=1, source_target_pairs={{0,2},{1,3},{2,0},{3,1},{4,6},{5,7},{6,4},{7,5},{8,10},{9,11},{10,... | collective-permute-start | bytes 442376 | tf_op jit(solution)/shard_map/ppermute | solution.py:26
  19.9 10.1 %collective-permute-start.4 = (bf16[4,32,576]{2,1,0:T(8,128)(2,1)S(1)}, bf16[4,32,576]{2,1,0:T(8,128)(2,1)S(1)}, u32[]{:S(2)}, u32[]{:S(2)}) collective-permute-start(bf16[4,32,576]{2,1,0:T(8,128)(2,1)S(1)} %join_slots.3.own_ref), channel_id=1, source_target_pairs={{0,4},{1,5},{2,6},{3,7},{4,0},{5,1},{6,2},{7,3},{8,12},{9,13},{10,... | collective-permute-start | bytes 442376 | tf_op jit(solution)/shard_map/ppermute | solution.py:26
  21.4 8.7 %collective-permute-start.6 = (bf16[4,32,576]{2,1,0:T(8,128)(2,1)S(1)}, bf16[4,32,576]{2,1,0:T(8,128)(2,1)S(1)}, u32[]{:S(2)}, u32[]{:S(2)}) collective-permute-start(bf16[4,32,576]{2,1,0:T(8,128)(2,1)S(1)} %join_slots.3.own_ref), channel_id=1, source_target_pairs={{0,6},{1,7},{2,4},{3,5},{4,2},{5,3},{6,0},{7,1},{8,14},{9,15},{10,... | collective-permute-start | bytes 442376 | tf_op jit(solution)/shard_map/ppermute | solution.py:26
  21.7 8.9 %collective-permute-start.8 = (bf16[4,32,576]{2,1,0:T(8,128)(2,1)S(1)}, bf16[4,32,576]{2,1,0:T(8,128)(2,1)S(1)}, u32[]{:S(2)}, u32[]{:S(2)}) collective-permute-start(bf16[4,32,576]{2,1,0:T(8,128)(2,1)S(1)} %join_slots.3.own_ref), channel_id=1, source_target_pairs={{0,1},{1,0},{2,3},{3,2},{4,5},{5,4},{6,7},{7,6},{8,9},{9,8},{10,11... | collective-permute-start | bytes 442376 | tf_op jit(solution)/shard_map/ppermute | solution.py:26
  26.6 7.1 %collective-permute-start.3 = (bf16[4,32,576]{2,1,0:T(8,128)(2,1)S(1)}, bf16[4,32,576]{2,1,0:T(8,128)(2,1)S(1)}, u32[]{:S(2)}, u32[]{:S(2)}) collective-permute-start(bf16[4,32,576]{2,1,0:T(8,128)(2,1)S(1)} %collective-permute-done.2.x_ref), channel_id=1, source_target_pairs={{0,1},{1,0},{2,3},{3,2},{4,5},{5,4},{6,7},{7,6},{8,9},{9,8},{10,11... | collective-permute-start | bytes 442376 | tf_op jit(solution)/shard_map/ppermute | solution.py:26
  30.1 3.7 %collective-permute-start.5 = (bf16[4,32,576]{2,1,0:T(8,128)(2,1)S(1)}, bf16[4,32,576]{2,1,0:T(8,128)(2,1)S(1)}, u32[]{:S(2)}, u32[]{:S(2)}) collective-permute-start(bf16[4,32,576]{2,1,0:T(8,128)(2,1)S(1)} %collective-permute-done.4.y_ref), channel_id=1, source_target_pairs={{0,1},{1,0},{2,3},{3,2},{4,5},{5,4},{6,7},{7,6},{8,9},{9,8},{10,11... | collective-permute-start | bytes 442376 | tf_op jit(solution)/shard_map/ppermute | solution.py:26
  30.1 3.7 %collective-permute-start.7 = (bf16[4,32,576]{2,1,0:T(8,128)(2,1)S(1)}, bf16[4,32,576]{2,1,0:T(8,128)(2,1)S(1)}, u32[]{:S(2)}, u32[]{:S(2)}) collective-permute-start(bf16[4,32,576]{2,1,0:T(8,128)(2,1)S(1)} %collective-permute-done.6.diagonal_ref), channel_id=1, source_target_pairs={{0,1},{1,0},{2,3},{3,2},{4,5},{5,4},{6,7},{7,6},{8,9},{9,8},{10,11... | collective-permute-start | bytes 442376 | tf_op jit(solution)/shard_map/ppermute | solution.py:26
